TPU v7x, 32 devices: a whole 2x2x4 slice. The times are simulated.
32 devices in a mesh: group: 2 (over x), tp: 16 (over z, y, core).
Axes of the slice: x: 2, y: 2, z: 4, core: 2. Of those that a mesh axis runs over, the one named last changes fastest.
Arguments:
- hidden_states: bfloat16 [16, 2, 8192], P('group'), parts along dimension 0, may hold values from -6 to 6
- qkv_weight: bfloat16 [10240, 8192], P('tp'), may hold values from -0.0625 to 0.0625
- out_weight: bfloat16 [8192, 8192], P('tp'), may hold values from -0.0625 to 0.0625
- cache_pages: bfloat16 [2048, 128, 256], P(('group', 'tp')), parts along dimension 0, may hold values from -6 to 6
- context_lengths: int32 [16], P('group'), parts along dimension 0, may hold values from 1 to 2046, 8184 in all
- new_units: int32 [128], P('group'), parts along dimension 0, may hold values from 0 to 63, as said below
- old_pages: int32 [2048], P('group'), parts along dimension 0, may hold values from 0 to 1023, as said below
Outputs:
- mixed_out: bfloat16 [16, 2, 8192], P('group', None, 'tp'), parts along dimension 0
- cache_out: bfloat16 [2048, 128, 256], P(('group', 'tp')), parts along dimension 0
There are 2 independent parts, one for each index of `group`. A program takes and returns all parts, laid end to end along the dimension named above; an argument that names none is the same for every part. Nothing has to cross between parts.
Inputs may be any that keep to these rules, and one draw needn't show every extreme that they name: `new_units`: A permutation of all request head groups; slot q of the new layout is on device q // 4. `old_pages`: A permutation of all logical pages (page u * 16 + i is page i of unit u); position p is on device p // 64. The pages that one device holds go to exactly 16 devices of the new layout, exactly 4 to each.
All inputs are finite; a program needn't handle non-finite values.
Results may differ from a plain program's by a relative error of at most 0.013.
Values may be sent and summed in bfloat16 or wider, within the bound.
A program may use at most 128 MiB of HBM per device.

v0:
```python
import math

import jax
import jax.numpy as jnp
from jax import lax
from jax.experimental import pallas as pl
from jax.experimental.pallas import tpu as pltpu
from jax.sharding import PartitionSpec as P

D = 8192
HEADS = 64
KVH = 8
HD = 128
U_DEV = 4
MAXCTX = 2048
PAGE = 128


rope_base = 10000.0


def rotate_positions(values, positions):
    half_dim = values.shape[-1] // 2
    frequency = rope_base ** (-(jnp.arange(half_dim, dtype=jnp.float32) * 2.0 / values.shape[-1]))
    angles = positions.astype(jnp.float32)[..., None] * frequency
    cosine = jnp.concatenate([jnp.cos(angles), jnp.cos(angles)], axis=-1)
    sine_table = jnp.concatenate([jnp.sin(angles), jnp.sin(angles)], axis=-1)
    turned = jnp.concatenate([-values[..., half_dim:], values[..., :half_dim]], axis=-1)
    return values * cosine + turned * sine_table


def prepare(unit_qkv, base_lengths):
    group_count = HEADS // KVH
    count_units = unit_qkv.shape[0]
    positions = base_lengths[:, None] + jnp.arange(2, dtype=jnp.int32)[None, :]
    widened = unit_qkv.astype(jnp.float32)
    queries = widened[..., : group_count * HD].reshape(count_units, 2, group_count, HD)
    queries = rotate_positions(queries, positions[:, :, None]).astype(jnp.bfloat16)
    new_keys = rotate_positions(
        widened[..., group_count * HD : (group_count + 1) * HD], positions
    ).astype(jnp.bfloat16)
    new_values = unit_qkv[..., (group_count + 1) * HD :]
    return (queries, new_keys, new_values)


def context_terms(context, queries, valid_count):
    score_scale = 1.0 / math.sqrt(HD)
    cached_keys = context[..., :HD]
    cached_values = context[..., HD:]
    scores = (
        jnp.einsum("psgd,ptd->psgt", queries, cached_keys, preferred_element_type=jnp.float32)
        * score_scale
    )
    visible = jnp.arange(context.shape[1], dtype=jnp.int32)[None, :] < valid_count[:, None]
    weights = jnp.where(visible[:, None, None, :], jnp.exp(scores), 0.0)
    totals = jnp.sum(weights, axis=-1)
    weighted = jnp.einsum(
        "psgt,ptd->psgd",
        weights.astype(jnp.bfloat16),
        cached_values,
        preferred_element_type=jnp.float32,
    )
    return (weighted, totals)


def own_terms(queries, new_keys, new_values):
    score_scale = 1.0 / math.sqrt(HD)
    scores = (
        jnp.einsum("usgd,ujd->usgj", queries, new_keys, preferred_element_type=jnp.float32)
        * score_scale
    )
    recent = jnp.arange(2, dtype=jnp.int32)[None, :] <= jnp.arange(2, dtype=jnp.int32)[:, None]
    weights = jnp.where(recent[None, :, None, :], jnp.exp(scores), 0.0)
    totals = jnp.sum(weights, axis=-1)
    weighted = jnp.einsum(
        "usgj,ujd->usgd",
        weights.astype(jnp.bfloat16),
        new_values,
        preferred_element_type=jnp.float32,
    )
    return (weighted, totals)


def plain_body(hidden_states, qkv_weight, out_weight, cache_pages, context_lengths, new_units, old_pages):
    devices = lax.axis_size("tp")
    device = lax.axis_index("tp")
    requests = hidden_states.shape[0]
    rows_dev = qkv_weight.shape[0]
    pages_dev, page_rows, page_width = cache_pages.shape
    group_count = HEADS // KVH
    unit_rows = (group_count + 2) * HD
    per_unit = MAXCTX // PAGE
    unit_slots = U_DEV
    capacity = max(1, pages_dev // devices)
    total_units = new_units.shape[0]
    total_pages = old_pages.shape[0]
    flat_rows = hidden_states.reshape(requests * 2, D)
    partial_qkv = lax.dot_general(
        flat_rows, qkv_weight, (((1,), (1,)), ((), ())), preferred_element_type=jnp.float32
    )
    partial_qkv = partial_qkv.astype(jnp.bfloat16).reshape(requests, 2, rows_dev)
    slot_index = (
        jnp.zeros((total_units,), jnp.int32)
        .at[new_units]
        .set(jnp.arange(total_units, dtype=jnp.int32))
    )
    own_units = lax.dynamic_slice_in_dim(new_units, device * unit_slots, unit_slots)
    own_requests = own_units // KVH
    own_heads = own_units % KVH
    own_lengths = context_lengths[own_requests]
    local_ids = lax.dynamic_slice_in_dim(old_pages, device * pages_dev, pages_dev)
    local_units = local_ids // per_unit
    local_index = local_ids % per_unit
    target_dev = (slot_index[local_units] * per_unit + local_index) // pages_dev
    local_order = jnp.arange(pages_dev, dtype=jnp.int32)
    send_rank = jnp.sum(
        (
            (target_dev[:, None] == target_dev[None, :])
            & (local_order[None, :] < local_order[:, None])
        ).astype(jnp.int32),
        axis=1,
    )
    outgoing = (
        jnp.zeros((devices, capacity, page_rows, page_width), jnp.bfloat16)
        .at[target_dev, send_rank]
        .set(cache_pages)
    )
    arrived = lax.all_to_all(outgoing, "tp", split_axis=0, concat_axis=0, tiled=True)
    stored_position = (
        jnp.zeros((total_pages,), jnp.int32)
        .at[old_pages]
        .set(jnp.arange(total_pages, dtype=jnp.int32))
    )
    wanted = (
        own_units[:, None] * per_unit + jnp.arange(per_unit, dtype=jnp.int32)[None, :]
    ).reshape(pages_dev)
    source_pos = stored_position[wanted]
    source_dev = source_pos // pages_dev
    source_slot = source_pos % pages_dev
    arrival_rank = jnp.sum(
        (
            (source_dev[:, None] == source_dev[None, :])
            & (source_slot[None, :] < source_slot[:, None])
        ).astype(jnp.int32),
        axis=1,
    )
    relaid = arrived[source_dev, arrival_rank]
    contexts = relaid.reshape(unit_slots, MAXCTX, page_width)
    sources_per_head = unit_rows // rows_dev
    request_table = (new_units // KVH).reshape(devices, unit_slots)
    outgoing_rows = partial_qkv[request_table]
    incoming = lax.all_to_all(outgoing_rows, "tp", split_axis=0, concat_axis=0, tiled=True)
    grouped = jnp.moveaxis(incoming.reshape(KVH, sources_per_head, unit_slots, 2, rows_dev), 2, 0)
    chosen = jnp.take_along_axis(grouped, own_heads[:, None, None, None, None], axis=1)[:, 0]
    own_rows = chosen.transpose(0, 2, 1, 3).reshape(unit_slots, 2, unit_rows)
    queries, new_keys, new_values = prepare(own_rows, own_lengths)
    cache_sums, cache_totals = context_terms(contexts, queries, own_lengths)
    own_sums, own_totals = own_terms(queries, new_keys, new_values)
    attended = ((cache_sums + own_sums) / (cache_totals + own_totals)[..., None]).astype(
        jnp.bfloat16
    )
    attended = attended.reshape(unit_slots, 2, group_count * HD)
    all_heads = lax.all_gather(attended, "tp", axis=0, tiled=True)
    logical = (
        all_heads[slot_index]
        .reshape(requests, KVH, 2, group_count * HD)
        .transpose(0, 2, 1, 3)
        .reshape(requests * 2, HEADS * HD)
    )
    mixed_rows = lax.dot_general(
        logical, out_weight, (((1,), (1,)), ((), ())), preferred_element_type=jnp.float32
    )
    mixed_rows = mixed_rows.astype(jnp.bfloat16).reshape(requests, 2, out_weight.shape[0])
    fresh_rows = jnp.concatenate([new_keys, new_values], axis=-1)
    positions = jnp.arange(MAXCTX, dtype=jnp.int32)[None, :]
    contexts = jnp.where(
        (positions == own_lengths[:, None])[..., None], fresh_rows[:, 0:1], contexts
    )
    contexts = jnp.where(
        (positions == own_lengths[:, None] + 1)[..., None], fresh_rows[:, 1:2], contexts
    )
    return (mixed_rows, contexts.reshape(pages_dev, page_rows, page_width))


def index_tables(context_lengths, new_units, old_pages, pages_dev):
    device = lax.axis_index("tp")
    per_unit = MAXCTX // PAGE
    total_units = new_units.shape[0]
    total_pages = old_pages.shape[0]
    capacity = pages_dev // lax.axis_size("tp")
    places = jnp.arange(pages_dev, dtype=jnp.int32)
    slots = jnp.arange(total_units, dtype=jnp.int32)

    def pick(hit, values):
        return jnp.sum(jnp.where(hit, values[None, :], 0), axis=1)

    def ranks(owner, order):
        before = (owner[:, None] == owner[None, :]) & (order[None, :] < order[:, None])
        return jnp.sum(before.astype(jnp.int32), axis=1)

    local_ids = lax.dynamic_slice_in_dim(old_pages, device * pages_dev, pages_dev)
    target_slot = pick((local_ids // per_unit)[:, None] == new_units[None, :], slots)
    target_dev = target_slot // U_DEV
    sent_at = target_dev * capacity + ranks(target_dev, places)
    sent = places[:, None] == sent_at[None, :]
    send_order = pick(sent, places)
    send_ids = pick(sent, local_ids)
    send_slot = pick(sent, target_slot % U_DEV)
    own_units = lax.dynamic_slice_in_dim(new_units, device * U_DEV, U_DEV)
    wanted = (
        own_units[:, None] * per_unit + jnp.arange(per_unit, dtype=jnp.int32)[None, :]
    ).reshape(pages_dev)
    source_pos = pick(
        wanted[:, None] == old_pages[None, :], jnp.arange(total_pages, dtype=jnp.int32)
    )
    source_dev = source_pos // pages_dev
    arrives_at = source_dev * capacity + ranks(source_dev, source_pos)
    slot_of_unit = pick(slots[:, None] == new_units[None, :], slots)
    requests = context_lengths.shape[0]
    send_units = send_ids // per_unit
    send_lengths = pick(
        (send_units // KVH)[:, None] == jnp.arange(requests, dtype=jnp.int32)[None, :],
        context_lengths,
    )
    send_left = send_lengths - (send_ids % per_unit) * PAGE
    send_query = (send_units % KVH) * requests + send_units // KVH
    own_heads, own_requests = own_units % KVH, own_units // KVH
    table = jnp.concatenate(
        [
            send_query, send_left, send_slot, slot_of_unit,
            own_heads * requests + own_requests, own_heads, own_requests,
        ]
    )
    return send_order, arrives_at, table


def sort_kernel(order_ref, pages_ref, out_ref, buf, in_sem, out_sem):
    count = buf.shape[0]

    def inward(i):
        return pltpu.make_async_copy(pages_ref.at[order_ref[i]], buf.at[i], in_sem.at[i])

    def outward(i):
        return pltpu.make_async_copy(buf.at[i], out_ref.at[i], out_sem.at[i])

    @pl.loop(0, count)
    def _(i):
        inward(i).start()

    @pl.loop(0, count)
    def _(i):
        inward(i).wait()
        outward(i).start()

    @pl.loop(0, count)
    def _(i):
        outward(i).wait()


def place_kernel(arrives_ref, lengths_ref, arrived_ref, fresh_ref, out_ref, buf, in_sem, out_sem):
    count = buf.shape[0]
    per_unit = MAXCTX // PAGE

    def inward(i):
        return pltpu.make_async_copy(arrived_ref.at[arrives_ref[i]], buf.at[i], in_sem.at[i])

    def outward(i):
        return pltpu.make_async_copy(buf.at[i], out_ref.at[i], out_sem.at[i])

    @pl.loop(0, count)
    def _(i):
        inward(i).start()

    @pl.loop(0, count)
    def _(i):
        inward(i).wait()
        slot = i // per_unit
        for step in range(2):
            position = lengths_ref[slot] + step

            @pl.when(position // PAGE == i % per_unit)
            def _():
                row = position % PAGE
                base = pl.multiple_of((row // 16) * 16, 16)
                tile = buf[i, pl.ds(base, 16), :]
                line = lax.broadcasted_iota(jnp.int32, tile.shape, 0)
                new = jnp.broadcast_to(fresh_ref[slot, step : step + 1, :], tile.shape)
                mixed = jnp.where(line == row - base, new, tile.astype(jnp.float32))
                buf[i, pl.ds(base, 16), :] = mixed.astype(jnp.bfloat16)

        outward(i).start()

    @pl.loop(0, count)
    def _(i):
        outward(i).wait()


NT = (((1,), (1,)), ((), ()))


def layer_kernel(
    devices, capacity,
    table, hidden_ref, cos_ref, sin_ref, qkv_hbm, out_hbm, pages_hbm,
    arrived_hbm, mixed_ref, fresh_ref,
    qkv_w, out_w, pages, rows_all, spread, queries, new_keys, new_values, part_out, part_in, swap_out, swap_in, att_all, flat,
    load_sem, page_send, page_recv, row_send, row_recv, part_send, part_recv, att_send, att_recv,
    self_sem,
):
    me = lax.axis_index("tp")
    pages_dev = pages.shape[0]
    rows = hidden_ref.shape[0]
    requests = rows // 2
    units = requests * KVH
    heads = qkv_w.shape[0]
    tiles = out_w.shape[0]
    group_count = HEADS // KVH
    head_rows = group_count + 2
    score_scale = 1.0 / math.sqrt(HD)
    span = requests * 2 * group_count
    at_left, at_target, at_slot = pages_dev, 2 * pages_dev, 3 * pages_dev
    at_own = at_slot + units
    at_head, at_request = at_own + U_DEV, at_own + 2 * U_DEV

    half = devices // 2
    here, side = lax.rem(me, half), me // half
    partner = lax.rem(me + half, devices)

    def near(offset):
        return side * half + lax.rem(here + offset, half)

    def near_sender(offset):
        return side * half + lax.rem(here + half - offset, half)

    def far(offset):
        return (1 - side) * half + lax.rem(here + offset, half)

    def far_sender(offset):
        return (1 - side) * half + lax.rem(here + half - offset, half)

    def remote(src, dst, send, recv, device):
        return pltpu.make_async_remote_copy(
            src_ref=src, dst_ref=dst, send_sem=send, recv_sem=recv,
            device_id={"tp": device}, device_id_type=pl.DeviceIdType.MESH,
        )

    def page_copy(rank, place, device):
        return remote(
            pages_hbm.at[device * capacity + rank], arrived_hbm.at[me * capacity + rank],
            page_send.at[rank, place], page_recv.at[rank, place], device,
        )

    def page_arrival(rank, place, device):
        at = device * capacity + rank
        return remote(
            pages_hbm.at[at], arrived_hbm.at[at],
            page_send.at[rank, place], page_recv.at[rank, place], device,
        )

    def row_copy(stage, place, owner, device):
        block = rows_all.at[owner]
        return remote(block, block, row_send.at[stage, place], row_recv.at[stage, place], device)

    def att_copy(stage, place, owner, device):
        block = att_all.at[pl.ds(owner * U_DEV, U_DEV)]
        return remote(block, block, att_send.at[stage, place], att_recv.at[stage, place], device)

    def part_copy(place, src, dst, device):
        return remote(
            part_out.at[src], part_in.at[dst], part_send.at[place], part_recv.at[place], device
        )

    def swap_copy():
        return remote(swap_out, swap_in, part_send.at[0], part_recv.at[0], partner)

    batches = 2 * capacity

    def send_pages(batch):
        if batch >= batches:
            return
        rank, low, high = batch // 2, (batch % 2) * (half // 2), (batch % 2 + 1) * (half // 2)
        if batch % 2:
            high = half

        if low == 0:
            page_copy(rank, 0, partner).start()

        @pl.loop(max(low, 1), high)
        def _(offset):
            page_copy(rank, offset, far(offset)).start()
            page_copy(rank, half + offset, near(offset)).start()

    def pack_totals(values):
        packed = jnp.zeros((2 * group_count, PAGE), jnp.float32)
        for j, total in enumerate(values):
            top = total.astype(jnp.bfloat16).astype(jnp.float32)
            packed = jnp.where(lane == j * strip, top, packed)
            packed = jnp.where(lane == j * strip + strip // 2, total - top, packed)
        return packed.astype(jnp.bfloat16)

    def unpack_total(packed, j):
        return jnp.sum(jnp.where(lane // strip == j, packed, 0.0), axis=-1, keepdims=True)

    lane = lax.broadcasted_iota(jnp.int32, (2 * group_count, PAGE), 1)
    strip = PAGE // U_DEV

    barrier = pltpu.get_barrier_semaphore()

    @pl.loop(1, devices)
    def _(offset):
        pl.semaphore_signal(
            barrier, inc=1, device_id={"tp": lax.rem(me + offset, devices)}, device_id_type=pl.DeviceIdType.MESH
        )

    loads = [
        pltpu.make_async_copy(qkv_hbm.at[pl.ds(c * HD, HD)], qkv_w.at[c], load_sem.at[c])
        for c in range(heads)
    ]
    loads.append(pltpu.make_async_copy(pages_hbm, pages, load_sem.at[heads]))
    loads += [
        pltpu.make_async_copy(
            out_hbm.at[pl.ds(c * HD, HD)], out_w.at[c], load_sem.at[heads + 1 + c]
        )
        for c in range(tiles)
    ]
    for load in loads[: heads + 1]:
        load.start()
    pl.semaphore_wait(barrier, devices - 1)
    send_pages(0)

    for c in range(heads):
        loads[c].wait()
        part = lax.dot_general(
            hidden_ref[...], qkv_w[c], NT, preferred_element_type=jnp.float32
        ).astype(jnp.bfloat16).astype(jnp.float32)
        turned = part * cos_ref[...] + pltpu.roll(part, HD // 2, 1) * sin_ref[...]
        is_value = lax.rem(me * heads + c, head_rows) == head_rows - 1
        rows_all[me, c] = jnp.where(is_value, part, turned).astype(jnp.bfloat16)

    row_copy(0, 0, me, partner).start()

    @pl.loop(1, half)
    def _(offset):
        row_copy(0, offset, me, near(offset)).start()

    send_pages(1)
    for load in loads[heads + 1 :]:
        load.start()
    loads[heads].wait()
    own_pages = pltpu.make_async_copy(
        pages.at[pl.ds(me * capacity, capacity)],
        arrived_hbm.at[pl.ds(me * capacity, capacity)],
        self_sem,
    )
    own_pages.start()

    row_copy(0, 0, partner, partner).wait_recv()

    @pl.loop(1, half)
    def _(offset):
        row_copy(1, offset, partner, near(offset)).start()

    send_pages(2)

    @pl.loop(1, half)
    def _(offset):
        source = near_sender(offset)
        row_copy(0, offset, source, source).wait_recv()
        row_copy(1, offset, lax.rem(source + half, devices), source).wait_recv()

    for h in range(KVH):
        for g in range(group_count):
            at = h * head_rows + g
            spread[pl.ds(h * span + g, rows, stride=group_count), :] = rows_all[
                at // heads, at % heads
            ].astype(jnp.float32)
        at = h * head_rows + group_count
        new_keys[h] = rows_all[at // heads, at % heads]
        new_values[h] = rows_all[(at + 1) // heads, (at + 1) % heads]
        for r in range(requests):
            start = h * span + r * 2 * group_count
            queries[h * requests + r] = spread[start : start + 2 * group_count, :].astype(
                jnp.bfloat16
            )

    @pl.loop(0, devices)
    def _(target):
        zero = jnp.zeros((2 * group_count, PAGE), jnp.float32)
        sums, totals = [zero] * U_DEV, [zero[:, :1]] * U_DEV
        for rank in range(capacity):
            query = queries[table[target * capacity + rank]]
            left = table[at_left + target * capacity + rank]
            page = pages[target * capacity + rank]
            scores = lax.dot_general(
                query, page[:, :HD], NT, preferred_element_type=jnp.float32
            ) * score_scale
            weights = jnp.where(lane < left, jnp.exp(scores), 0.0)
            total = jnp.sum(weights, axis=-1, keepdims=True)
            weighted = jnp.dot(
                weights.astype(jnp.bfloat16), page[:, HD:], preferred_element_type=jnp.float32
            )
            slot = table[at_target + target * capacity + rank]
            for j in range(U_DEV):
                sums[j] = sums[j] + jnp.where(slot == j, weighted, 0.0)
                totals[j] = totals[j] + jnp.where(slot == j, total, 0.0)
        place, which = lax.rem(target, half), target // half
        for j in range(U_DEV):
            part_out[place, which, j] = sums[j].astype(jnp.bfloat16)
        part_out[place, which, U_DEV] = pack_totals(totals)

    @pl.loop(1, half)
    def _(offset):
        part_copy(offset, lax.rem(here + offset, half), here, near(offset)).start()

    send_pages(3)

    own_sums, own_totals = [], []
    row = lax.broadcasted_iota(jnp.int32, (2 * group_count, rows), 0)
    col = lax.broadcasted_iota(jnp.int32, (2 * group_count, rows), 1)
    line = lax.broadcasted_iota(jnp.int32, (rows, HD), 0)
    for j in range(U_DEV):
        request = table[at_request + j]
        keys = new_keys[table[at_head + j]]
        values = new_values[table[at_head + j]]
        scores = lax.dot_general(
            queries[table[at_own + j]], keys, NT, preferred_element_type=jnp.float32
        ) * score_scale
        seen = (col // 2 == request) & (col % 2 <= row // group_count)
        weights = jnp.where(seen, jnp.exp(scores), 0.0)
        own_totals.append(jnp.sum(weights, axis=-1, keepdims=True))
        own_sums.append(
            jnp.dot(weights.astype(jnp.bfloat16), values, preferred_element_type=jnp.float32)
        )
        for step in range(2):
            mine = line == request * 2 + step
            for part, kind in ((0, keys), (1, values)):
                fresh_ref[j, step : step + 1, part * HD : (part + 1) * HD] = jnp.sum(
                    jnp.where(mine, kind.astype(jnp.float32), 0.0), axis=0, keepdims=True
                )

    @pl.loop(1, half)
    def _(offset):
        source = near_sender(offset)
        part_copy(offset, here, lax.rem(here + half - offset, half), source).wait_recv()

    def half_sum(which):
        def add(offset, carry):
            block = part_in.at[lax.rem(here + offset, half), which]
            return tuple(c + block[j].astype(jnp.float32) for j, c in enumerate(carry))

        first = tuple(
            part_out[here, which, j].astype(jnp.float32) for j in range(U_DEV + 1)
        )
        return lax.fori_loop(1, half, add, first)

    away = half_sum(1 - side)
    for j in range(U_DEV):
        swap_out[j] = away[j].astype(jnp.bfloat16)
    swap_out[U_DEV] = pack_totals([unpack_total(away[U_DEV], j) for j in range(U_DEV)])
    kept = half_sum(side)
    swap_copy().start()
    send_pages(4)
    swap_copy().wait_recv()
    packed = kept[U_DEV] + swap_in[U_DEV].astype(jnp.float32)
    for j in range(U_DEV):
        total = own_totals[j] + unpack_total(packed, j)
        weighted = own_sums[j] + kept[j] + swap_in[j].astype(jnp.float32)
        att_all[me * U_DEV + j] = (weighted / total).astype(jnp.bfloat16)

    att_copy(0, 0, me, partner).start()

    @pl.loop(1, half)
    def _(offset):
        att_copy(0, offset, me, near(offset)).start()

    send_pages(5)
    att_copy(0, 0, partner, partner).wait_recv()

    @pl.loop(1, half)
    def _(offset):
        att_copy(1, offset, partner, near(offset)).start()

    for batch in range(6, batches):
        send_pages(batch)

    @pl.loop(1, half)
    def _(offset):
        source = near_sender(offset)
        att_copy(0, offset, source, source).wait_recv()
        att_copy(1, offset, lax.rem(source + half, devices), source).wait_recv()

    for r in range(requests):
        for h in range(KVH):
            slot = table[at_slot + r * KVH + h]
            spread[h * span + r * 2 * group_count : h * span + (r + 1) * 2 * group_count, :] = (
                att_all[slot].astype(jnp.float32)
            )
    for h in range(KVH):
        for g in range(group_count):
            at = (h * group_count + g) * HD
            flat[:, at : at + HD] = spread[
                pl.ds(h * span + g, rows, stride=group_count), :
            ].astype(jnp.bfloat16)
    for c in range(tiles):
        loads[heads + 1 + c].wait()
        mixed_ref[:, c * HD : (c + 1) * HD] = lax.dot_general(
            flat[...], out_w[c], NT, preferred_element_type=jnp.float32
        ).astype(jnp.bfloat16)

    own_pages.wait()

    row_copy(0, 0, me, partner).wait_send()
    att_copy(0, 0, me, partner).wait_send()
    swap_copy().wait_send()

    @pl.loop(1, half)
    def _(offset):
        for stage, owner in ((0, me), (1, partner)):
            row_copy(stage, offset, owner, near(offset)).wait_send()
            att_copy(stage, offset, owner, near(offset)).wait_send()
        part_copy(offset, lax.rem(here + offset, half), here, near(offset)).wait_send()

    for rank in range(capacity):
        page_copy(rank, 0, partner).wait_send()
        page_arrival(rank, 0, partner).wait_recv()

        @pl.loop(1, half)
        def _(offset):
            page_copy(rank, offset, far(offset)).wait_send()
            page_arrival(rank, offset, far_sender(offset)).wait_recv()
            page_copy(rank, half + offset, near(offset)).wait_send()
            page_arrival(rank, half + offset, near_sender(offset)).wait_recv()


def fused_body(hidden_states, qkv_weight, out_weight, cache_pages, context_lengths, new_units, old_pages):
    devices = lax.axis_size("tp")
    requests = hidden_states.shape[0]
    rows = requests * 2
    pages_dev = cache_pages.shape[0]
    capacity = pages_dev // devices
    heads = qkv_weight.shape[0] // HD
    tiles = out_weight.shape[0] // HD
    group_count = HEADS // KVH
    units = new_units.shape[0]
    hbm = pl.BlockSpec(memory_space=pl.ANY)
    vmem = pl.BlockSpec(memory_space=pltpu.VMEM)
    smem = pl.BlockSpec(memory_space=pltpu.SMEM)
    dma = pltpu.SemaphoreType.DMA
    send_order, arrives_at, table = index_tables(
        context_lengths, new_units, old_pages, pages_dev
    )
    positions = (
        context_lengths[:, None] + jnp.arange(2, dtype=jnp.int32)[None, :]
    ).reshape(rows).astype(jnp.float32)
    half = HD // 2
    frequency = rope_base ** (-(jnp.arange(half, dtype=jnp.float32) * 2.0 / HD))
    angles = positions[:, None] * frequency
    cosine, sine = jnp.cos(angles), jnp.sin(angles)
    cosine = jnp.concatenate([cosine, cosine], axis=-1)
    sine = jnp.concatenate([-sine, sine], axis=-1)

    buffers = [
        pltpu.VMEM(cache_pages.shape, jnp.bfloat16), dma((pages_dev,)), dma((pages_dev,)),
    ]
    outgoing = pl.pallas_call(
        sort_kernel,
        out_shape=jax.ShapeDtypeStruct(cache_pages.shape, jnp.bfloat16),
        in_specs=[smem, hbm],
        out_specs=hbm,
        scratch_shapes=buffers,
        name="sort_pages",
    )(send_order, cache_pages)
    tile = (2 * group_count, HD)
    arrived, mixed, fresh = pl.pallas_call(
        lambda *refs: layer_kernel(devices, capacity, *refs),
        out_shape=(
            jax.ShapeDtypeStruct(cache_pages.shape, jnp.bfloat16),
            jax.ShapeDtypeStruct((rows, out_weight.shape[0]), jnp.bfloat16),
            jax.ShapeDtypeStruct((U_DEV, 2, 2 * HD), jnp.float32),
        ),
        in_specs=[smem, vmem, vmem, vmem, hbm, hbm, hbm],
        out_specs=(hbm, vmem, vmem),
        scratch_shapes=[
            pltpu.VMEM((heads, HD, D), jnp.bfloat16),
            pltpu.VMEM((tiles, HD, HEADS * HD), jnp.bfloat16),
            pltpu.VMEM(cache_pages.shape, jnp.bfloat16),
            pltpu.VMEM((devices, heads, rows, HD), jnp.bfloat16),
            pltpu.VMEM((units * 2 * group_count, HD), jnp.float32),
            pltpu.VMEM((units,) + tile, jnp.bfloat16),
            pltpu.VMEM((KVH, rows, HD), jnp.bfloat16),
            pltpu.VMEM((KVH, rows, HD), jnp.bfloat16),
            pltpu.VMEM((devices // 2, 2, U_DEV + 1) + tile, jnp.bfloat16),
            pltpu.VMEM((devices // 2, 2, U_DEV + 1) + tile, jnp.bfloat16),
            pltpu.VMEM((U_DEV + 1,) + tile, jnp.bfloat16),
            pltpu.VMEM((U_DEV + 1,) + tile, jnp.bfloat16),
            pltpu.VMEM((units,) + tile, jnp.bfloat16),
            pltpu.VMEM((rows, HEADS * HD), jnp.bfloat16),
            dma((heads + 1 + tiles,)),
            dma((capacity, devices)), dma((capacity, devices)),
            dma((2, devices // 2)), dma((2, devices // 2)),
            dma((devices // 2,)), dma((devices // 2,)),
            dma((2, devices // 2)), dma((2, devices // 2)),
            dma(()),
        ],
        compiler_params=pltpu.CompilerParams(
            collective_id=0, has_side_effects=True, vmem_limit_bytes=48 << 20
        ),
        name="layer",
    )(table, hidden_states.reshape(rows, D), cosine, sine, qkv_weight, out_weight, outgoing)
    own_lengths = jnp.take(
        context_lengths,
        lax.dynamic_slice_in_dim(new_units, lax.axis_index("tp") * U_DEV, U_DEV) // KVH,
    )
    placed = pl.pallas_call(
        place_kernel,
        out_shape=jax.ShapeDtypeStruct(cache_pages.shape, jnp.bfloat16),
        in_specs=[smem, smem, hbm, vmem],
        out_specs=hbm,
        scratch_shapes=buffers,
        name="place_pages",
    )(arrives_at, own_lengths, arrived, fresh)
    return (mixed.reshape(requests, 2, out_weight.shape[0]), placed)


def body(hidden_states, qkv_weight, out_weight, cache_pages, context_lengths, new_units, old_pages):
    devices = lax.axis_size("tp")
    whole_heads = qkv_weight.shape[0] % HD == 0 and out_weight.shape[0] % HD == 0
    whole_shares = cache_pages.shape[0] % devices == 0 and devices % 4 == 0 and hidden_states.shape[0] == KVH
    chosen = fused_body if whole_heads and whole_shares else plain_body
    return chosen(
        hidden_states, qkv_weight, out_weight, cache_pages, context_lengths, new_units, old_pages
    )


def solution(mesh):
    in_specs = (
        P("group", None, None),
        P("tp", None),
        P("tp", None),
        P(("group", "tp"), None, None),
        P("group"),
        P("group"),
        P("group"),
    )
    out_specs = (P("group", None, "tp"), P(("group", "tp"), None, None))
    return jax.shard_map(body, mesh=mesh, in_specs=in_specs, out_specs=out_specs, check_vma=False)
```

profile of v0, /device:TPU:1, one launch (start us, length us, event | category | flops | bytes accessed | tf_op | source)
XLA Modules:
  0.0 132.0 jit_solution(7510570502371101558)
XLA Ops:
  0.6 0.8 and_select_fusion.10
  1.4 0.8 select_reduce_fusion.2
  2.3 0.2 convert_reduce_fusion.1
  2.5 0.6 select_reduce_fusion.1
  3.1 0.7 select_reduce_fusion.6
  3.9 0.7 compare_select_fusion
  4.6 0.1 iota_add_fusion
  4.7 0.1 add.138
  4.8 0.9 select_reduce_fusion
  5.7 0.2 convert_reduce_fusion
  5.9 0.6 multiply_add_fusion.arrives_ref
  6.5 1.3 gather_fusion
  7.8 0.5 multiply_add_fusion.1
  8.3 0.1 concatenate.9.refs_0_
  8.4 0.7 add_convert_fusion
  9.1 0.1 convert_element_type.18
  9.2 0.1 fusion.1
  9.3 0.1 pad_maximum_fusion
  9.4 1.1 reshape.179.refs_1_
  10.5 5.8 %sort_pages.1.refs_6_ = bf16[64,128,256]{2,1,0:T(8,128)(2,1)} custom-call(s32[64]{0:T(128)} %get-tuple-element.8.order_ref, bf16[64,128,256]{2,1,0:T(8,128)(2,1)} %pages_ref.1), custom_call_target="tpu_custom_call" | custom-call | tf_op jit(solution)/shard_map/sort_pages/pallas_call | solution.py:664
  16.3 106.4 %layer.1 = (bf16[64,128,256]{2,1,0:T(8,128)(2,1)S(1)}, bf16[16,512]{1,0:T(8,128)(2,1)S(1)}, f32[4,2,256]{2,1,0:T(2,128)S(1)}) custom-call(s32[268]{0:T(512)S(1)} %concatenate.9.refs_0_, bf16[16,8192]{1,0:T(8,128)(2,1)S(1)} %reshape.179.refs_1_, f32[16,128]{1,0:T(8,128)S(1)} %get-tuple-element.29.refs_2_, f32[16,128]{1,0:T(8,128)S(1)} %get-tuple-element.30.refs_3_, ...), custom_call_target="tpu_custom_call" | custom-call | tf_op jit(solution)/shard_map/layer/pallas_call | solution.py:673
  122.7 0.0 copy-start
  122.7 1.9 %copy-done = bf16[64,128,256]{2,1,0:T(8,128)(2,1)} copy-done((bf16[64,128,256]{2,1,0:T(8,128)(2,1)}, bf16[64,128,256]{2,1,0:T(8,128)(2,1)S(1)}, u32[]{:S(2)}) %copy-start) | copy-done | bytes 4194328
  124.7 0.0 copy-start.1
  124.7 0.6 copy-done.1
  125.3 0.6 reshape.180
  125.9 6.1 %place_pages.1 = bf16[64,128,256]{2,1,0:T(8,128)(2,1)} custom-call(s32[64]{0:T(128)} %multiply_add_fusion.arrives_ref, s32[4]{0:T(128)} %get-tuple-element.25.lengths_ref, bf16[64,128,256]{2,1,0:T(8,128)(2,1)} %copy-done, f32[4,2,256]{2,1,0:T(2,128)} %copy-done.1), custom_call_target="tpu_custom_call" | custom-call | tf_op jit(solution)/shard_map/place_pages/pallas_call | solution.py:713
  (7 shorter events, 0.1 us)
Async XLA Ops:
  122.7 1.9 %copy-start = (bf16[64,128,256]{2,1,0:T(8,128)(2,1)}, bf16[64,128,256]{2,1,0:T(8,128)(2,1)S(1)}, u32[]{:S(2)}) copy-start(bf16[64,128,256]{2,1,0:T(8,128)(2,1)S(1)} %get-tuple-element.6.arrived_ref) | copy-start | bytes 12582916
  124.7 0.6 copy-start.1
where the time goes:
time: 132 us
  Pallas kernels  118 us (89%)
  other arithmetic  7.19 us (5%)
  local copies, waits for them, and re-layouts  5.72 us (4%)
    pallas_call x1, Pallas kernels, fused_body(): pl.pallas_call(lambda *refs: layer_kernel(devices, capacity, *refs), out_...  106 us
    pallas_call x1, Pallas kernels, fused_body(): pl.pallas_call(place_kernel, out_shape=jax.ShapeDtypeStruct(cache_pages.s...  6.15 us
    pallas_call x1, Pallas kernels, fused_body(): pl.pallas_call(sort_kernel, out_shape=jax.ShapeDtypeStruct(cache_pages.sh...  5.83 us
    reduce_sum x4, other arithmetic, pick(): return jnp.sum(jnp.where(hit, values[None, :], 0), axis=1)  3.09 us

commit v1 on v0

--- a/solution.py
+++ b/solution.py
@@ -182,117 +182,64 @@
     return (mixed_rows, contexts.reshape(pages_dev, page_rows, page_width))
 
 
-def index_tables(context_lengths, new_units, old_pages, pages_dev):
-    device = lax.axis_index("tp")
+def place_kernel(
+    table_ref, arrived_ref, fresh_ref, mixed_ref, out_ref, rows_ref, patched, rows, sem, rows_sem
+):
+    count = out_ref.shape[0]
     per_unit = MAXCTX // PAGE
-    total_units = new_units.shape[0]
-    total_pages = old_pages.shape[0]
-    capacity = pages_dev // lax.axis_size("tp")
-    places = jnp.arange(pages_dev, dtype=jnp.int32)
-    slots = jnp.arange(total_units, dtype=jnp.int32)
-
-    def pick(hit, values):
-        return jnp.sum(jnp.where(hit, values[None, :], 0), axis=1)
-
-    def ranks(owner, order):
-        before = (owner[:, None] == owner[None, :]) & (order[None, :] < order[:, None])
-        return jnp.sum(before.astype(jnp.int32), axis=1)
-
-    local_ids = lax.dynamic_slice_in_dim(old_pages, device * pages_dev, pages_dev)
-    target_slot = pick((local_ids // per_unit)[:, None] == new_units[None, :], slots)
-    target_dev = target_slot // U_DEV
-    sent_at = target_dev * capacity + ranks(target_dev, places)
-    sent = places[:, None] == sent_at[None, :]
-    send_order = pick(sent, places)
-    send_ids = pick(sent, local_ids)
-    send_slot = pick(sent, target_slot % U_DEV)
-    own_units = lax.dynamic_slice_in_dim(new_units, device * U_DEV, U_DEV)
-    wanted = (
-        own_units[:, None] * per_unit + jnp.arange(per_unit, dtype=jnp.int32)[None, :]
-    ).reshape(pages_dev)
-    source_pos = pick(
-        wanted[:, None] == old_pages[None, :], jnp.arange(total_pages, dtype=jnp.int32)
-    )
-    source_dev = source_pos // pages_dev
-    arrives_at = source_dev * capacity + ranks(source_dev, source_pos)
-    slot_of_unit = pick(slots[:, None] == new_units[None, :], slots)
-    requests = context_lengths.shape[0]
-    send_units = send_ids // per_unit
-    send_lengths = pick(
-        (send_units // KVH)[:, None] == jnp.arange(requests, dtype=jnp.int32)[None, :],
-        context_lengths,
-    )
-    send_left = send_lengths - (send_ids % per_unit) * PAGE
-    send_query = (send_units % KVH) * requests + send_units // KVH
-    own_heads, own_requests = own_units % KVH, own_units // KVH
-    table = jnp.concatenate(
-        [
-            send_query, send_left, send_slot, slot_of_unit,
-            own_heads * requests + own_requests, own_heads, own_requests,
-        ]
-    )
-    return send_order, arrives_at, table
-
-
-def sort_kernel(order_ref, pages_ref, out_ref, buf, in_sem, out_sem):
-    count = buf.shape[0]
-
-    def inward(i):
-        return pltpu.make_async_copy(pages_ref.at[order_ref[i]], buf.at[i], in_sem.at[i])
-
-    def outward(i):
-        return pltpu.make_async_copy(buf.at[i], out_ref.at[i], out_sem.at[i])
+    steps = fresh_ref.shape[1]
+
+    def outward(i, src):
+        return pltpu.make_async_copy(src, out_ref.at[i], sem.at[i])
+
+    def written(slot, step):
+        return (table_ref[1, slot] + step) // PAGE
 
     @pl.loop(0, count)
     def _(i):
-        inward(i).start()
+        slot, page = i // per_unit, i % per_unit
+
+        @pl.when((written(slot, 0) != page) & (written(slot, 1) != page))
+        def _():
+            outward(i, arrived_ref.at[table_ref[0, i]]).start()
+
+    for slot in range(U_DEV):
+        for step in range(steps):
+            page = written(slot, step)
+            at = slot * per_unit + page
+            block = patched.at[slot, step]
+            block[...] = arrived_ref[table_ref[0, at]]
+            for other in range(steps):
+                row = table_ref[1, slot] + other - page * PAGE
+
+                @pl.when((row >= 0) & (row < PAGE))
+                def _():
+                    base = pl.multiple_of((row // 16) * 16, 16)
+                    tile = block[pl.ds(base, 16), :]
+                    line = lax.broadcasted_iota(jnp.int32, tile.shape, 0)
+                    new = jnp.broadcast_to(fresh_ref[slot, other : other + 1, :], tile.shape)
+                    mixed = jnp.where(line == row - base, new, tile.astype(jnp.float32))
+                    block[pl.ds(base, 16), :] = mixed.astype(jnp.bfloat16)
+
+            if step == 0:
+                outward(at, block).start()
+            else:
+
+                @pl.when(page != written(slot, 0))
+                def _():
+                    outward(at, block).start()
+
+    mixed = mixed_ref[...].astype(jnp.float32)
+    for r in range(rows.shape[0]):
+        rows[r] = mixed[2 * r : 2 * r + 2].astype(jnp.bfloat16)
+    rows_out = pltpu.make_async_copy(rows, rows_ref, rows_sem)
+    rows_out.start()
 
     @pl.loop(0, count)
     def _(i):
-        inward(i).wait()
-        outward(i).start()
-
-    @pl.loop(0, count)
-    def _(i):
-        outward(i).wait()
-
-
-def place_kernel(arrives_ref, lengths_ref, arrived_ref, fresh_ref, out_ref, buf, in_sem, out_sem):
-    count = buf.shape[0]
-    per_unit = MAXCTX // PAGE
-
-    def inward(i):
-        return pltpu.make_async_copy(arrived_ref.at[arrives_ref[i]], buf.at[i], in_sem.at[i])
-
-    def outward(i):
-        return pltpu.make_async_copy(buf.at[i], out_ref.at[i], out_sem.at[i])
-
-    @pl.loop(0, count)
-    def _(i):
-        inward(i).start()
-
-    @pl.loop(0, count)
-    def _(i):
-        inward(i).wait()
-        slot = i // per_unit
-        for step in range(2):
-            position = lengths_ref[slot] + step
-
-            @pl.when(position // PAGE == i % per_unit)
-            def _():
-                row = position % PAGE
-                base = pl.multiple_of((row // 16) * 16, 16)
-                tile = buf[i, pl.ds(base, 16), :]
-                line = lax.broadcasted_iota(jnp.int32, tile.shape, 0)
-                new = jnp.broadcast_to(fresh_ref[slot, step : step + 1, :], tile.shape)
-                mixed = jnp.where(line == row - base, new, tile.astype(jnp.float32))
-                buf[i, pl.ds(base, 16), :] = mixed.astype(jnp.bfloat16)
-
-        outward(i).start()
-
-    @pl.loop(0, count)
-    def _(i):
-        outward(i).wait()
+        outward(i, arrived_ref.at[0]).wait()
+
+    rows_out.wait()
 
 
 NT = (((1,), (1,)), ((), ()))
@@ -300,26 +247,26 @@
 
 def layer_kernel(
     devices, capacity,
-    table, hidden_ref, cos_ref, sin_ref, qkv_hbm, out_hbm, pages_hbm,
-    arrived_hbm, mixed_ref, fresh_ref,
-    qkv_w, out_w, pages, rows_all, spread, queries, new_keys, new_values, part_out, part_in, swap_out, swap_in, att_all, flat,
+    lengths_hbm, units_hbm, ids_hbm, hidden_hbm, qkv_hbm, out_hbm, pages_hbm,
+    arrived_hbm, mixed_ref, fresh_ref, place_ref,
+    lengths, units_s, units_v, ids, tables_v, table, hidden_in, hidden_wide, hidden_ref, cos_ref, sin_ref,
+    qkv_w, out_w, unsorted, pages, rows_all, spread, queries, new_keys, new_values, part_out, part_in, swap_out, swap_in, att_all, flat,
     load_sem, page_send, page_recv, row_send, row_recv, part_send, part_recv, att_send, att_recv,
-    self_sem,
+    self_sem, small_sem, table_sem,
 ):
     me = lax.axis_index("tp")
     pages_dev = pages.shape[0]
     rows = hidden_ref.shape[0]
     requests = rows // 2
     units = requests * KVH
+    per_unit = MAXCTX // PAGE
     heads = qkv_w.shape[0]
     tiles = out_w.shape[0]
     group_count = HEADS // KVH
     head_rows = group_count + 2
     score_scale = 1.0 / math.sqrt(HD)
     span = requests * 2 * group_count
-    at_left, at_target, at_slot = pages_dev, 2 * pages_dev, 3 * pages_dev
-    at_own = at_slot + units
-    at_head, at_request = at_own + U_DEV, at_own + 2 * U_DEV
+    in_order, of_query, of_left, of_target, of_slot = range(5)
 
     half = devices // 2
     here, side = lax.rem(me, half), me // half
@@ -345,14 +292,14 @@
 
     def page_copy(rank, place, device):
         return remote(
-            pages_hbm.at[device * capacity + rank], arrived_hbm.at[me * capacity + rank],
+            pages.at[device * capacity + rank], arrived_hbm.at[me * capacity + rank],
             page_send.at[rank, place], page_recv.at[rank, place], device,
         )
 
     def page_arrival(rank, place, device):
         at = device * capacity + rank
         return remote(
-            pages_hbm.at[at], arrived_hbm.at[at],
+            pages.at[at], arrived_hbm.at[at],
             page_send.at[rank, place], page_recv.at[rank, place], device,
         )
 
@@ -411,21 +358,103 @@
             barrier, inc=1, device_id={"tp": lax.rem(me + offset, devices)}, device_id_type=pl.DeviceIdType.MESH
         )
 
+    small = [
+        pltpu.make_async_copy(ids_hbm, ids, small_sem.at[0]),
+        pltpu.make_async_copy(units_hbm, units_v, small_sem.at[1]),
+        pltpu.make_async_copy(units_hbm, units_s, small_sem.at[2]),
+        pltpu.make_async_copy(lengths_hbm, lengths, small_sem.at[3]),
+    ]
+    load_pages = pltpu.make_async_copy(pages_hbm, unsorted, small_sem.at[4])
+    load_hidden = pltpu.make_async_copy(hidden_hbm, hidden_in, small_sem.at[5])
     loads = [
         pltpu.make_async_copy(qkv_hbm.at[pl.ds(c * HD, HD)], qkv_w.at[c], load_sem.at[c])
         for c in range(heads)
     ]
-    loads.append(pltpu.make_async_copy(pages_hbm, pages, load_sem.at[heads]))
     loads += [
         pltpu.make_async_copy(
-            out_hbm.at[pl.ds(c * HD, HD)], out_w.at[c], load_sem.at[heads + 1 + c]
+            out_hbm.at[pl.ds(c * HD, HD)], out_w.at[c], load_sem.at[heads + c]
         )
         for c in range(tiles)
     ]
-    for load in loads[: heads + 1]:
+    for load in small + [load_pages, load_hidden] + loads[:heads]:
         load.start()
+
+    def numbers(shape, axis):
+        return lax.broadcasted_iota(jnp.int32, shape, axis)
+
+    def whole(values, size):
+        return lax.shift_right_logical(values, jnp.full_like(values, size.bit_length() - 1))
+
+    def index_row(values, size):
+        return jnp.clip(values, 0, size - 1)
+
+    def down(hit, values):
+        return jnp.sum(jnp.where(hit, values, 0), axis=0, keepdims=True)
+
+    def across(hit, values):
+        return jnp.sum(jnp.where(hit, values, 0), axis=1, keepdims=True)
+
+    square = (pages_dev, pages_dev)
+    k_sub, k_lane = numbers(square, 0), numbers(square, 1)
+    small[0].wait()
+    first = me * pages_dev
+    wide = (pages_dev, ids.shape[1])
+    own_ids = ids[pl.ds(first // ids.shape[1], 1), :]
+    mine = numbers(wide, 1) == numbers(wide, 0) + lax.rem(first, ids.shape[1])
+    id_col = across(mine, own_ids)
+    small[1].wait()
+    unit_row = units_v[...]
+    by_unit = (pages_dev, units)
+    slot_col = across(whole(id_col, per_unit) == unit_row, numbers(by_unit, 1))
+    target_col = whole(slot_col, U_DEV)
+    target_row = down(k_sub == k_lane, target_col)
+    rank_col = across((target_col == target_row) & (k_lane < k_sub), jnp.ones(square, jnp.int32))
+    sent = target_col * capacity + rank_col == k_lane
+    tables_v[in_order : in_order + 1, :] = index_row(down(sent, k_sub), pages_dev)
+    id_row = down(sent, id_col)
+    tables_v[of_target : of_target + 1, :] = down(sent, slot_col - target_col * U_DEV)
+    sent_unit = whole(id_row, per_unit)
+    sent_request = whole(sent_unit, KVH)
+    small[3].wait()
+    sent_length = jnp.zeros_like(id_row)
+    for r in range(requests):
+        sent_length = jnp.where(sent_request == r, lengths[0, r], sent_length)
+    tables_v[of_query : of_query + 1, :] = index_row(
+        (sent_unit - sent_request * KVH) * requests + sent_request, units
+    )
+    tables_v[of_left : of_left + 1, :] = sent_length - (id_row - sent_unit * per_unit) * PAGE
+    u_square = (units, units)
+    u_sub, u_lane = numbers(u_square, 0), numbers(u_square, 1)
+    unit_col = across(u_sub == u_lane, unit_row)
+    tables_v[of_slot : of_slot + 1, :] = index_row(down(unit_col == u_lane, u_sub), units)
+    to_table = pltpu.make_async_copy(tables_v, table, table_sem.at[0])
+    to_table.start()
+
+    load_pages.wait()
+    to_table.wait()
+
+    @pl.loop(0, pages_dev)
+    def _(i):
+        pages[i] = unsorted[table[in_order, i]]
+
     pl.semaphore_wait(barrier, devices - 1)
     send_pages(0)
+
+    small[2].wait()
+    row_at = lax.broadcasted_iota(jnp.int32, (rows, HD), 0)
+    lane_at = lax.broadcasted_iota(jnp.int32, (rows, HD), 1)
+    positions = jnp.zeros((rows, HD), jnp.float32)
+    for r in range(requests):
+        positions = jnp.where(row_at // 2 == r, lengths[0, r].astype(jnp.float32), positions)
+    positions = positions + (row_at % 2).astype(jnp.float32)
+    power = (lane_at % (HD // 2)).astype(jnp.float32) * (2.0 / HD)
+    angles = positions * jnp.exp(power * -math.log(rope_base))
+    cos_ref[...] = jnp.cos(angles)
+    sin_ref[...] = jnp.where(lane_at < HD // 2, -jnp.sin(angles), jnp.sin(angles))
+    load_hidden.wait()
+    for r in range(requests):
+        hidden_wide[2 * r : 2 * r + 2, :] = hidden_in[r].astype(jnp.float32)
+    hidden_ref[...] = hidden_wide[...].astype(jnp.bfloat16)
 
     for c in range(heads):
         loads[c].wait()
@@ -443,9 +472,8 @@
         row_copy(0, offset, me, near(offset)).start()
 
     send_pages(1)
-    for load in loads[heads + 1 :]:
+    for load in loads[heads:]:
         load.start()
-    loads[heads].wait()
     own_pages = pltpu.make_async_copy(
         pages.at[pl.ds(me * capacity, capacity)],
         arrived_hbm.at[pl.ds(me * capacity, capacity)],
@@ -487,8 +515,8 @@
         zero = jnp.zeros((2 * group_count, PAGE), jnp.float32)
         sums, totals = [zero] * U_DEV, [zero[:, :1]] * U_DEV
         for rank in range(capacity):
-            query = queries[table[target * capacity + rank]]
-            left = table[at_left + target * capacity + rank]
+            query = queries[table[of_query, target * capacity + rank]]
+            left = table[of_left, target * capacity + rank]
             page = pages[target * capacity + rank]
             scores = lax.dot_general(
                 query, page[:, :HD], NT, preferred_element_type=jnp.float32
@@ -498,7 +526,7 @@
             weighted = jnp.dot(
                 weights.astype(jnp.bfloat16), page[:, HD:], preferred_element_type=jnp.float32
             )
-            slot = table[at_target + target * capacity + rank]
+            slot = table[of_target, target * capacity + rank]
             for j in range(U_DEV):
                 sums[j] = sums[j] + jnp.where(slot == j, weighted, 0.0)
                 totals[j] = totals[j] + jnp.where(slot == j, total, 0.0)
@@ -518,11 +546,12 @@
     col = lax.broadcasted_iota(jnp.int32, (2 * group_count, rows), 1)
     line = lax.broadcasted_iota(jnp.int32, (rows, HD), 0)
     for j in range(U_DEV):
-        request = table[at_request + j]
-        keys = new_keys[table[at_head + j]]
-        values = new_values[table[at_head + j]]
+        unit = units_s[0, me * U_DEV + j]
+        request, head = unit // KVH, unit % KVH
+        keys = new_keys[head]
+        values = new_values[head]
         scores = lax.dot_general(
-            queries[table[at_own + j]], keys, NT, preferred_element_type=jnp.float32
+            queries[head * requests + request], keys, NT, preferred_element_type=jnp.float32
         ) * score_scale
         seen = (col // 2 == request) & (col % 2 <= row // group_count)
         weights = jnp.where(seen, jnp.exp(scores), 0.0)
@@ -536,6 +565,33 @@
                 fresh_ref[j, step : step + 1, part * HD : (part + 1) * HD] = jnp.sum(
                     jnp.where(mine, kind.astype(jnp.float32), 0.0), axis=0, keepdims=True
                 )
+
+    slot_at = numbers((pages_dev, 1), 0)
+    wanted = jnp.zeros((pages_dev, 1), jnp.int32)
+    for j in range(U_DEV):
+        first_page = units_s[0, me * U_DEV + j] * per_unit - j * per_unit
+        wanted = jnp.where(whole(slot_at, per_unit) == j, slot_at + first_page, wanted)
+    found = jnp.zeros(wide, jnp.int32)
+    for b in range(ids.shape[0]):
+        found = found + jnp.where(
+            wanted == ids[b : b + 1, :], numbers(wide, 1) + b * wide[1], 0
+        )
+    source_col = jnp.sum(found, axis=1, keepdims=True)
+    source_row = down(k_sub == k_lane, source_col)
+    holder_col, holder_row = whole(source_col, pages_dev), whole(source_row, pages_dev)
+    rank_col = across(
+        (holder_col == holder_row) & (source_row < source_col), jnp.ones(square, jnp.int32)
+    )
+    place_ref[0:1, :] = index_row(
+        down(k_sub == k_lane, holder_col * capacity + rank_col), pages_dev
+    )
+    own_lengths = jnp.zeros((1, pages_dev), jnp.int32)
+    for j in range(U_DEV):
+        own_lengths = jnp.where(
+            lax.broadcasted_iota(jnp.int32, (1, pages_dev), 1) == j,
+            lengths[0, units_s[0, me * U_DEV + j] // KVH], own_lengths,
+        )
+    place_ref[1:2, :] = own_lengths
 
     @pl.loop(1, half)
     def _(offset):
@@ -590,7 +646,7 @@
 
     for r in range(requests):
         for h in range(KVH):
-            slot = table[at_slot + r * KVH + h]
+            slot = table[of_slot, r * KVH + h]
             spread[h * span + r * 2 * group_count : h * span + (r + 1) * 2 * group_count, :] = (
                 att_all[slot].astype(jnp.float32)
             )
@@ -601,7 +657,7 @@
                 pl.ds(h * span + g, rows, stride=group_count), :
             ].astype(jnp.bfloat16)
     for c in range(tiles):
-        loads[heads + 1 + c].wait()
+        loads[heads + c].wait()
         mixed_ref[:, c * HD : (c + 1) * HD] = lax.dot_general(
             flat[...], out_w[c], NT, preferred_element_type=jnp.float32
         ).astype(jnp.bfloat16)
@@ -645,86 +701,86 @@
     vmem = pl.BlockSpec(memory_space=pltpu.VMEM)
     smem = pl.BlockSpec(memory_space=pltpu.SMEM)
     dma = pltpu.SemaphoreType.DMA
-    send_order, arrives_at, table = index_tables(
-        context_lengths, new_units, old_pages, pages_dev
-    )
-    positions = (
-        context_lengths[:, None] + jnp.arange(2, dtype=jnp.int32)[None, :]
-    ).reshape(rows).astype(jnp.float32)
-    half = HD // 2
-    frequency = rope_base ** (-(jnp.arange(half, dtype=jnp.float32) * 2.0 / HD))
-    angles = positions[:, None] * frequency
-    cosine, sine = jnp.cos(angles), jnp.sin(angles)
-    cosine = jnp.concatenate([cosine, cosine], axis=-1)
-    sine = jnp.concatenate([-sine, sine], axis=-1)
-
-    buffers = [
-        pltpu.VMEM(cache_pages.shape, jnp.bfloat16), dma((pages_dev,)), dma((pages_dev,)),
-    ]
-    outgoing = pl.pallas_call(
-        sort_kernel,
-        out_shape=jax.ShapeDtypeStruct(cache_pages.shape, jnp.bfloat16),
-        in_specs=[smem, hbm],
-        out_specs=hbm,
-        scratch_shapes=buffers,
-        name="sort_pages",
-    )(send_order, cache_pages)
+    lengths = context_lengths.reshape(1, requests)
+    unit_table = new_units.reshape(1, units)
+    page_table = old_pages.reshape(-1, PAGE)
     tile = (2 * group_count, HD)
-    arrived, mixed, fresh = pl.pallas_call(
+    f32, bf16, i32 = jnp.float32, jnp.bfloat16, jnp.int32
+    arrived, mixed, fresh, place = pl.pallas_call(
         lambda *refs: layer_kernel(devices, capacity, *refs),
         out_shape=(
-            jax.ShapeDtypeStruct(cache_pages.shape, jnp.bfloat16),
-            jax.ShapeDtypeStruct((rows, out_weight.shape[0]), jnp.bfloat16),
-            jax.ShapeDtypeStruct((U_DEV, 2, 2 * HD), jnp.float32),
+            jax.ShapeDtypeStruct(cache_pages.shape, bf16),
+            jax.ShapeDtypeStruct((rows, out_weight.shape[0]), bf16),
+            jax.ShapeDtypeStruct((U_DEV, 2, 2 * HD), f32),
+            jax.ShapeDtypeStruct((2, pages_dev), i32),
         ),
-        in_specs=[smem, vmem, vmem, vmem, hbm, hbm, hbm],
-        out_specs=(hbm, vmem, vmem),
+        in_specs=[pl.BlockSpec(memory_space=pltpu.HBM)] * 7,
+        out_specs=(hbm, vmem, vmem, vmem),
         scratch_shapes=[
-            pltpu.VMEM((heads, HD, D), jnp.bfloat16),
-            pltpu.VMEM((tiles, HD, HEADS * HD), jnp.bfloat16),
-            pltpu.VMEM(cache_pages.shape, jnp.bfloat16),
-            pltpu.VMEM((devices, heads, rows, HD), jnp.bfloat16),
-            pltpu.VMEM((units * 2 * group_count, HD), jnp.float32),
-            pltpu.VMEM((units,) + tile, jnp.bfloat16),
-            pltpu.VMEM((KVH, rows, HD), jnp.bfloat16),
-            pltpu.VMEM((KVH, rows, HD), jnp.bfloat16),
-            pltpu.VMEM((devices // 2, 2, U_DEV + 1) + tile, jnp.bfloat16),
-            pltpu.VMEM((devices // 2, 2, U_DEV + 1) + tile, jnp.bfloat16),
-            pltpu.VMEM((U_DEV + 1,) + tile, jnp.bfloat16),
-            pltpu.VMEM((U_DEV + 1,) + tile, jnp.bfloat16),
-            pltpu.VMEM((units,) + tile, jnp.bfloat16),
-            pltpu.VMEM((rows, HEADS * HD), jnp.bfloat16),
-            dma((heads + 1 + tiles,)),
+            pltpu.SMEM(lengths.shape, i32),
+            pltpu.SMEM(unit_table.shape, i32),
+            pltpu.VMEM(unit_table.shape, i32),
+            pltpu.VMEM(page_table.shape, i32),
+            pltpu.VMEM((8, pages_dev), i32),
+            pltpu.SMEM((8, pages_dev), i32),
+            pltpu.VMEM(hidden_states.shape, bf16),
+            pltpu.VMEM((rows, D), f32),
+            pltpu.VMEM((rows, D), bf16),
+            pltpu.VMEM((rows, HD), f32),
+            pltpu.VMEM((rows, HD), f32),
+            pltpu.VMEM((heads, HD, D), bf16),
+            pltpu.VMEM((tiles, HD, HEADS * HD), bf16),
+            pltpu.VMEM(cache_pages.shape, bf16),
+            pltpu.VMEM(cache_pages.shape, bf16),
+            pltpu.VMEM((devices, heads, rows, HD), bf16),
+            pltpu.VMEM((units * 2 * group_count, HD), f32),
+            pltpu.VMEM((units,) + tile, bf16),
+            pltpu.VMEM((KVH, rows, HD), bf16),
+            pltpu.VMEM((KVH, rows, HD), bf16),
+            pltpu.VMEM((devices // 2, 2, U_DEV + 1) + tile, bf16),
+            pltpu.VMEM((devices // 2, 2, U_DEV + 1) + tile, bf16),
+            pltpu.VMEM((U_DEV + 1,) + tile, bf16),
+            pltpu.VMEM((U_DEV + 1,) + tile, bf16),
+            pltpu.VMEM((units,) + tile, bf16),
+            pltpu.VMEM((rows, HEADS * HD), bf16),
+            dma((heads + tiles,)),
             dma((capacity, devices)), dma((capacity, devices)),
             dma((2, devices // 2)), dma((2, devices // 2)),
             dma((devices // 2,)), dma((devices // 2,)),
             dma((2, devices // 2)), dma((2, devices // 2)),
-            dma(()),
+            dma(()), dma((6,)), dma((1,)),
         ],
         compiler_params=pltpu.CompilerParams(
-            collective_id=0, has_side_effects=True, vmem_limit_bytes=48 << 20
+            collective_id=0, has_side_effects=True, vmem_limit_bytes=44 << 20
         ),
         name="layer",
-    )(table, hidden_states.reshape(rows, D), cosine, sine, qkv_weight, out_weight, outgoing)
-    own_lengths = jnp.take(
-        context_lengths,
-        lax.dynamic_slice_in_dim(new_units, lax.axis_index("tp") * U_DEV, U_DEV) // KVH,
-    )
-    placed = pl.pallas_call(
+    )(*[pltpu.with_memory_space_constraint(x, pltpu.HBM) for x in (lengths, unit_table, page_table, hidden_states, qkv_weight, out_weight, cache_pages)])
+    mixed_shape = (requests, 2, out_weight.shape[0])
+    placed, mixed = pl.pallas_call(
         place_kernel,
-        out_shape=jax.ShapeDtypeStruct(cache_pages.shape, jnp.bfloat16),
-        in_specs=[smem, smem, hbm, vmem],
-        out_specs=hbm,
-        scratch_shapes=buffers,
+        out_shape=(
+            jax.ShapeDtypeStruct(cache_pages.shape, bf16),
+            jax.ShapeDtypeStruct(mixed_shape, bf16),
+        ),
+        in_specs=[smem, vmem, vmem, vmem],
+        out_specs=(hbm, hbm),
+        scratch_shapes=[
+            pltpu.VMEM((U_DEV, 2) + cache_pages.shape[1:], bf16),
+            pltpu.VMEM(mixed_shape, bf16),
+            dma((pages_dev,)), dma(()),
+        ],
+        compiler_params=pltpu.CompilerParams(vmem_limit_bytes=8 << 20),
         name="place_pages",
-    )(arrives_at, own_lengths, arrived, fresh)
-    return (mixed.reshape(requests, 2, out_weight.shape[0]), placed)
+    )(place, arrived, fresh, mixed)
+    return (mixed, placed)
 
 
 def body(hidden_states, qkv_weight, out_weight, cache_pages, context_lengths, new_units, old_pages):
     devices = lax.axis_size("tp")
     whole_heads = qkv_weight.shape[0] % HD == 0 and out_weight.shape[0] % HD == 0
-    whole_shares = cache_pages.shape[0] % devices == 0 and devices % 4 == 0 and hidden_states.shape[0] == KVH
+    pages_dev = cache_pages.shape[0]
+    whole_shares = pages_dev % devices == 0 and devices % 4 == 0 and hidden_states.shape[0] == KVH
+    whole_shares = whole_shares and new_units.shape[0] == pages_dev and PAGE % pages_dev == 0
     chosen = fused_body if whole_heads and whole_shares else plain_body
     return chosen(
         hidden_states, qkv_weight, out_weight, cache_pages, context_lengths, new_units, old_pages

time: 132 us -> 113 us (0.86)
  other arithmetic: 7.19 us -> 0 us
  Pallas kernels: 118 us -> 112 us
  local copies, waits for them, and re-layouts: 5.72 us -> 0 us
    pallas_call x2 -> x1, Pallas kernels: 12 us -> 4.06 us  [fused_body(): pl.pallas_call(place_kernel, out_shape=(jax.ShapeDtypeStruct(cache_pages....]
    reduce_sum x6 -> x0, other arithmetic: 3.45 us -> none  [the longest x4 3.09 us: pick(): return jnp.sum(jnp.where(hit, values[None, :], 0), axis=1)]
    unnamed x4 -> x0, local copies, waits for them, and re-layouts: 2.51 us -> none
    pallas_call x1, Pallas kernels: 106 us -> 108 us  [fused_body(): pl.pallas_call(lambda *refs: layer_kernel(devices, capacity, *refs), out_...]
    reshape x2 -> x0, local copies, waits for them, and re-layouts: 1.67 us -> none  [the longest x1 1.05 us: fused_body(): hidden_states.reshape(rows, D)]
    select_n x4 -> x0, other arithmetic: 1.53 us -> none  [the longest x1 0.77 us: index_tables(): local_ids // per_unit]
where the time goes in v1:
time: 113 us
  Pallas kernels  112 us (99%)
    pallas_call x1, Pallas kernels, fused_body(): pl.pallas_call(lambda *refs: layer_kernel(devices, capacity, *refs), out_...  108 us
    pallas_call x1, Pallas kernels, fused_body(): pl.pallas_call(place_kernel, out_shape=(jax.ShapeDtypeStruct(cache_pages....  4.06 us

profile of v1, /device:TPU:1, one launch (start us, length us, event | category | flops | bytes accessed | tf_op | source)
XLA Modules:
  0.0 112.9 jit_solution(2816641093133515656)
XLA Ops:
  0.6 108.2 %layer.1 = (bf16[64,128,256]{2,1,0:T(8,128)(2,1)S(1)}, bf16[16,512]{1,0:T(8,128)(2,1)S(1)}, f32[4,2,256]{2,1,0:T(2,128)S(1)}, s32[2,64]{1,0:T(2,128)S(1)}) custom-call(s32[1,8]{1,0:T(1,128)} %bitcast.4, s32[1,64]{1,0:T(1,128)} %bitcast.5, s32[8,128]{1,0:T(8,128)} %bitcast.3, bf16[8,2,8192]{2,1,0:T(2,128)(2,1)} %refs_3_.1, bf16[640,8192]{1,0:T(8,128)(2,1)} %refs_4_.1, ...), custom_call_target="tpu_custom_call" | custom-call | tf_op jit(solution)/shard_map/layer/pallas_call | solution.py:709
  108.8 4.1 %place_pages.1 = (bf16[64,128,256]{2,1,0:T(8,128)(2,1)}, bf16[8,2,512]{2,1,0:T(2,128)(2,1)}) custom-call(s32[2,64]{1,0:T(2,128)S(1)} %get-tuple-element.8.table_ref, bf16[64,128,256]{2,1,0:T(8,128)(2,1)S(1)} %get-tuple-element.9.arrived_ref, f32[4,2,256]{2,1,0:T(2,128)S(1)} %get-tuple-element.10.fresh_ref, bf16[16,512]{1,0:T(8,128)(2,1)S(1)} %get-tuple-element.11.mixed_ref), custom_call_target="tpu_custom_call" | custom-call | tf_op jit(solution)/shard_map/place_pages/pallas_call | solution.py:759

commit v2 on v1

--- a/solution.py
+++ b/solution.py
@@ -185,74 +185,60 @@
 def place_kernel(
     table_ref, arrived_ref, fresh_ref, mixed_ref, out_ref, rows_ref, patched, rows, sem, rows_sem
 ):
-    count = out_ref.shape[0]
     per_unit = MAXCTX // PAGE
     steps = fresh_ref.shape[1]
 
-    def outward(i, src):
-        return pltpu.make_async_copy(src, out_ref.at[i], sem.at[i])
-
-    def written(slot, step):
-        return (table_ref[1, slot] + step) // PAGE
-
-    @pl.loop(0, count)
-    def _(i):
-        slot, page = i // per_unit, i % per_unit
-
-        @pl.when((written(slot, 0) != page) & (written(slot, 1) != page))
-        def _():
-            outward(i, arrived_ref.at[table_ref[0, i]]).start()
+    def outward(at, src):
+        return pltpu.make_async_copy(src, out_ref.at[at], sem)
+
+    def place_of(slot, page):
+        return slot * per_unit + lax.rem(table_ref[1, slot] // PAGE + page, per_unit)
 
     for slot in range(U_DEV):
-        for step in range(steps):
-            page = written(slot, step)
-            at = slot * per_unit + page
-            block = patched.at[slot, step]
+        for page in range(steps, per_unit):
+            at = place_of(slot, page)
+            outward(at, arrived_ref.at[table_ref[0, at]]).start()
+
+    for slot in range(U_DEV):
+        for page in range(steps):
+            at = place_of(slot, page)
+            block = patched.at[slot, page]
             block[...] = arrived_ref[table_ref[0, at]]
-            for other in range(steps):
-                row = table_ref[1, slot] + other - page * PAGE
+            for step in range(steps):
+                row = table_ref[1, slot] + step - (at - slot * per_unit) * PAGE
 
                 @pl.when((row >= 0) & (row < PAGE))
                 def _():
                     base = pl.multiple_of((row // 16) * 16, 16)
                     tile = block[pl.ds(base, 16), :]
                     line = lax.broadcasted_iota(jnp.int32, tile.shape, 0)
-                    new = jnp.broadcast_to(fresh_ref[slot, other : other + 1, :], tile.shape)
+                    new = jnp.broadcast_to(fresh_ref[slot, step : step + 1, :], tile.shape)
                     mixed = jnp.where(line == row - base, new, tile.astype(jnp.float32))
                     block[pl.ds(base, 16), :] = mixed.astype(jnp.bfloat16)
 
-            if step == 0:
-                outward(at, block).start()
-            else:
-
-                @pl.when(page != written(slot, 0))
-                def _():
-                    outward(at, block).start()
+            outward(at, block).start()
 
     mixed = mixed_ref[...].astype(jnp.float32)
     for r in range(rows.shape[0]):
         rows[r] = mixed[2 * r : 2 * r + 2].astype(jnp.bfloat16)
     rows_out = pltpu.make_async_copy(rows, rows_ref, rows_sem)
     rows_out.start()
-
-    @pl.loop(0, count)
-    def _(i):
-        outward(i, arrived_ref.at[0]).wait()
-
+    pltpu.make_async_copy(arrived_ref, out_ref, sem).wait()
     rows_out.wait()
 
 
 NT = (((1,), (1,)), ((), ()))
+PLAN = (4, 8, 12, 18, 24)
 
 
 def layer_kernel(
     devices, capacity,
     lengths_hbm, units_hbm, ids_hbm, hidden_hbm, qkv_hbm, out_hbm, pages_hbm,
-    arrived_hbm, mixed_ref, fresh_ref, place_ref,
+    arrived_hbm, mixed_hbm, fresh_hbm, place_hbm,
     lengths, units_s, units_v, ids, tables_v, table, hidden_in, hidden_wide, hidden_ref, cos_ref, sin_ref,
     qkv_w, out_w, unsorted, pages, rows_all, spread, queries, new_keys, new_values, part_out, part_in, swap_out, swap_in, att_all, flat,
-    load_sem, page_send, page_recv, row_send, row_recv, part_send, part_recv, att_send, att_recv,
-    self_sem, small_sem, table_sem,
+    load_sem, page_send, page_recv, row_send, row_recv, part_send, part_recv, swap_send, swap_recv, att_send, att_recv,
+    small_sem, table_sem, mixed_ref, fresh_ref, place_ref, result_sem,
 ):
     me = lax.axis_index("tp")
     pages_dev = pages.shape[0]
@@ -268,21 +254,15 @@
     span = requests * 2 * group_count
     in_order, of_query, of_left, of_target, of_slot = range(5)
 
-    half = devices // 2
+    half, quarter = devices // 2, devices // 4
     here, side = lax.rem(me, half), me // half
     partner = lax.rem(me + half, devices)
 
     def near(offset):
         return side * half + lax.rem(here + offset, half)
 
-    def near_sender(offset):
-        return side * half + lax.rem(here + half - offset, half)
-
-    def far(offset):
-        return (1 - side) * half + lax.rem(here + offset, half)
-
-    def far_sender(offset):
-        return (1 - side) * half + lax.rem(here + half - offset, half)
+    def far(turn):
+        return (1 - side) * half + (turn // quarter) * quarter + lax.rem(turn + me, quarter)
 
     def remote(src, dst, send, recv, device):
         return pltpu.make_async_remote_copy(
@@ -290,51 +270,53 @@
             device_id={"tp": device}, device_id_type=pl.DeviceIdType.MESH,
         )
 
-    def page_copy(rank, place, device):
+    def page_copy(rank, device):
         return remote(
             pages.at[device * capacity + rank], arrived_hbm.at[me * capacity + rank],
-            page_send.at[rank, place], page_recv.at[rank, place], device,
-        )
-
-    def page_arrival(rank, place, device):
-        at = device * capacity + rank
+            page_send, page_recv, device,
+        )
+
+    def row_copy(kind, owner, device):
+        block = rows_all.at[owner]
+        return remote(block, block, row_send, row_recv.at[kind], device)
+
+    def many_rows(count):
+        blocks = rows_all.at[pl.ds(0, count)]
+        return remote(blocks, blocks, row_send, row_recv.at[1], partner)
+
+    def att_copy(device):
+        block = att_all.at[here]
+        return remote(block, block, att_send, att_recv, device)
+
+    def many_att(count):
+        blocks = att_all.at[pl.ds(0, count)]
+        return remote(blocks, blocks, att_send, att_recv, partner)
+
+    def part_copy(src, dst, device):
+        return remote(part_out.at[src], part_in.at[dst], part_send, part_recv, device)
+
+    def many_parts(count):
         return remote(
-            pages.at[at], arrived_hbm.at[at],
-            page_send.at[rank, place], page_recv.at[rank, place], device,
-        )
-
-    def row_copy(stage, place, owner, device):
-        block = rows_all.at[owner]
-        return remote(block, block, row_send.at[stage, place], row_recv.at[stage, place], device)
-
-    def att_copy(stage, place, owner, device):
-        block = att_all.at[pl.ds(owner * U_DEV, U_DEV)]
-        return remote(block, block, att_send.at[stage, place], att_recv.at[stage, place], device)
-
-    def part_copy(place, src, dst, device):
-        return remote(
-            part_out.at[src], part_in.at[dst], part_send.at[place], part_recv.at[place], device
+            part_out.at[pl.ds(0, count)], part_in.at[pl.ds(0, count)], part_send, part_recv, partner
         )
 
     def swap_copy():
-        return remote(swap_out, swap_in, part_send.at[0], part_recv.at[0], partner)
-
-    batches = 2 * capacity
-
-    def send_pages(batch):
-        if batch >= batches:
-            return
-        rank, low, high = batch // 2, (batch % 2) * (half // 2), (batch % 2 + 1) * (half // 2)
-        if batch % 2:
-            high = half
-
-        if low == 0:
-            page_copy(rank, 0, partner).start()
-
-        @pl.loop(max(low, 1), high)
-        def _(offset):
-            page_copy(rank, offset, far(offset)).start()
-            page_copy(rank, half + offset, near(offset)).start()
+        return remote(swap_out, swap_in, swap_send, swap_recv, partner)
+
+    turns = half * capacity
+
+    def send_pages(start, stop):
+        @pl.loop(start, stop)
+        def _(turn):
+            rank, place = turn // half, lax.rem(turn, half)
+            page_copy(rank, far(place)).start()
+
+            @pl.when(place > 0)
+            def _():
+                page_copy(rank, near(place)).start()
+
+    def share(numerator):
+        return turns * numerator // 32
 
     def pack_totals(values):
         packed = jnp.zeros((2 * group_count, PAGE), jnp.float32)
@@ -376,7 +358,7 @@
         )
         for c in range(tiles)
     ]
-    for load in small + [load_pages, load_hidden] + loads[:heads]:
+    for load in small + [load_pages]:
         load.start()
 
     def numbers(shape, axis):
@@ -426,11 +408,16 @@
     u_square = (units, units)
     u_sub, u_lane = numbers(u_square, 0), numbers(u_square, 1)
     unit_col = across(u_sub == u_lane, unit_row)
-    tables_v[of_slot : of_slot + 1, :] = index_row(down(unit_col == u_lane, u_sub), units)
+    u_device = whole(u_sub, U_DEV)
+    u_side = whole(u_device, half)
+    u_place = (u_device - u_side * half) * (2 * U_DEV) + u_side * U_DEV + (u_sub - u_device * U_DEV)
+    tables_v[of_slot : of_slot + 1, :] = index_row(down(unit_col == u_lane, u_place), units)
     to_table = pltpu.make_async_copy(tables_v, table, table_sem.at[0])
     to_table.start()
 
     load_pages.wait()
+    for load in [load_hidden] + loads[:heads]:
+        load.start()
     to_table.wait()
 
     @pl.loop(0, pages_dev)
@@ -438,7 +425,7 @@
         pages[i] = unsorted[table[in_order, i]]
 
     pl.semaphore_wait(barrier, devices - 1)
-    send_pages(0)
+    send_pages(0, share(PLAN[0]))
 
     small[2].wait()
     row_at = lax.broadcasted_iota(jnp.int32, (rows, HD), 0)
@@ -465,35 +452,31 @@
         is_value = lax.rem(me * heads + c, head_rows) == head_rows - 1
         rows_all[me, c] = jnp.where(is_value, part, turned).astype(jnp.bfloat16)
 
-    row_copy(0, 0, me, partner).start()
+    row_copy(0, me, partner).start()
 
     @pl.loop(1, half)
     def _(offset):
-        row_copy(0, offset, me, near(offset)).start()
-
-    send_pages(1)
+        row_copy(1, me, near(offset)).start()
+
+    send_pages(share(PLAN[0]), share(PLAN[1]))
     for load in loads[heads:]:
         load.start()
     own_pages = pltpu.make_async_copy(
         pages.at[pl.ds(me * capacity, capacity)],
         arrived_hbm.at[pl.ds(me * capacity, capacity)],
-        self_sem,
+        page_recv,
     )
     own_pages.start()
 
-    row_copy(0, 0, partner, partner).wait_recv()
+    row_copy(0, partner, partner).wait_recv()
 
     @pl.loop(1, half)
     def _(offset):
-        row_copy(1, offset, partner, near(offset)).start()
-
-    send_pages(2)
-
-    @pl.loop(1, half)
-    def _(offset):
-        source = near_sender(offset)
-        row_copy(0, offset, source, source).wait_recv()
-        row_copy(1, offset, lax.rem(source + half, devices), source).wait_recv()
+        row_copy(1, partner, near(offset)).start()
+
+    send_pages(share(PLAN[1]), share(PLAN[2]))
+
+    many_rows(devices - 2).wait_recv()
 
     for h in range(KVH):
         for g in range(group_count):
@@ -512,6 +495,11 @@
 
     @pl.loop(0, devices)
     def _(target):
+        spent = share(PLAN[3]) - share(PLAN[2])
+        send_pages(
+            share(PLAN[2]) + target * spent // devices,
+            share(PLAN[2]) + (target + 1) * spent // devices,
+        )
         zero = jnp.zeros((2 * group_count, PAGE), jnp.float32)
         sums, totals = [zero] * U_DEV, [zero[:, :1]] * U_DEV
         for rank in range(capacity):
@@ -537,31 +525,30 @@
 
     @pl.loop(1, half)
     def _(offset):
-        part_copy(offset, lax.rem(here + offset, half), here, near(offset)).start()
-
-    send_pages(3)
+        part_copy(lax.rem(here + offset, half), here, near(offset)).start()
 
     own_sums, own_totals = [], []
     row = lax.broadcasted_iota(jnp.int32, (2 * group_count, rows), 0)
     col = lax.broadcasted_iota(jnp.int32, (2 * group_count, rows), 1)
     line = lax.broadcasted_iota(jnp.int32, (rows, HD), 0)
-    for j in range(U_DEV):
-        unit = units_s[0, me * U_DEV + j]
+    for j in range(2 * U_DEV):
+        unit = units_s[0, (j // U_DEV * half + here) * U_DEV + j % U_DEV]
         request, head = unit // KVH, unit % KVH
-        keys = new_keys[head]
-        values = new_values[head]
         scores = lax.dot_general(
-            queries[head * requests + request], keys, NT, preferred_element_type=jnp.float32
+            queries[head * requests + request], new_keys[head], NT, preferred_element_type=jnp.float32
         ) * score_scale
         seen = (col // 2 == request) & (col % 2 <= row // group_count)
         weights = jnp.where(seen, jnp.exp(scores), 0.0)
         own_totals.append(jnp.sum(weights, axis=-1, keepdims=True))
         own_sums.append(
-            jnp.dot(weights.astype(jnp.bfloat16), values, preferred_element_type=jnp.float32)
-        )
+            jnp.dot(weights.astype(jnp.bfloat16), new_values[head], preferred_element_type=jnp.float32)
+        )
+    for j in range(U_DEV):
+        unit = units_s[0, me * U_DEV + j]
+        request, head = unit // KVH, unit % KVH
         for step in range(2):
             mine = line == request * 2 + step
-            for part, kind in ((0, keys), (1, values)):
+            for part, kind in ((0, new_keys[head]), (1, new_values[head])):
                 fresh_ref[j, step : step + 1, part * HD : (part + 1) * HD] = jnp.sum(
                     jnp.where(mine, kind.astype(jnp.float32), 0.0), axis=0, keepdims=True
                 )
@@ -593,10 +580,7 @@
         )
     place_ref[1:2, :] = own_lengths
 
-    @pl.loop(1, half)
-    def _(offset):
-        source = near_sender(offset)
-        part_copy(offset, here, lax.rem(here + half - offset, half), source).wait_recv()
+    many_parts(half - 1).wait_recv()
 
     def half_sum(which):
         def add(offset, carry):
@@ -608,47 +592,39 @@
         )
         return lax.fori_loop(1, half, add, first)
 
-    away = half_sum(1 - side)
-    for j in range(U_DEV):
-        swap_out[j] = away[j].astype(jnp.bfloat16)
-    swap_out[U_DEV] = pack_totals([unpack_total(away[U_DEV], j) for j in range(U_DEV)])
-    kept = half_sum(side)
+    kept = half_sum(0) + half_sum(1)
+    blocks = U_DEV + 1
+    for which in range(2):
+        for j in range(U_DEV):
+            swap_out[which * blocks + j] = kept[which * blocks + j].astype(jnp.bfloat16)
+        packed = kept[which * blocks + U_DEV]
+        swap_out[which * blocks + U_DEV] = pack_totals(
+            [unpack_total(packed, j) for j in range(U_DEV)]
+        )
     swap_copy().start()
-    send_pages(4)
+    send_pages(share(PLAN[3]), share(PLAN[4]))
     swap_copy().wait_recv()
-    packed = kept[U_DEV] + swap_in[U_DEV].astype(jnp.float32)
-    for j in range(U_DEV):
-        total = own_totals[j] + unpack_total(packed, j)
-        weighted = own_sums[j] + kept[j] + swap_in[j].astype(jnp.float32)
-        att_all[me * U_DEV + j] = (weighted / total).astype(jnp.bfloat16)
-
-    att_copy(0, 0, me, partner).start()
+    for which in range(2):
+        last = which * blocks + U_DEV
+        packed = kept[last] + swap_in[last].astype(jnp.float32)
+        for j in range(U_DEV):
+            at = which * blocks + j
+            total = own_totals[which * U_DEV + j] + unpack_total(packed, j)
+            weighted = own_sums[which * U_DEV + j] + kept[at] + swap_in[at].astype(jnp.float32)
+            att_all[here, which * U_DEV + j] = (weighted / total).astype(jnp.bfloat16)
 
     @pl.loop(1, half)
     def _(offset):
-        att_copy(0, offset, me, near(offset)).start()
-
-    send_pages(5)
-    att_copy(0, 0, partner, partner).wait_recv()
-
-    @pl.loop(1, half)
-    def _(offset):
-        att_copy(1, offset, partner, near(offset)).start()
-
-    for batch in range(6, batches):
-        send_pages(batch)
-
-    @pl.loop(1, half)
-    def _(offset):
-        source = near_sender(offset)
-        att_copy(0, offset, source, source).wait_recv()
-        att_copy(1, offset, lax.rem(source + half, devices), source).wait_recv()
+        att_copy(near(offset)).start()
+
+    send_pages(share(PLAN[4]), turns)
+    many_att(half - 1).wait_recv()
 
     for r in range(requests):
         for h in range(KVH):
             slot = table[of_slot, r * KVH + h]
             spread[h * span + r * 2 * group_count : h * span + (r + 1) * 2 * group_count, :] = (
-                att_all[slot].astype(jnp.float32)
+                att_all[slot // (2 * U_DEV), slot % (2 * U_DEV)].astype(jnp.float32)
             )
     for h in range(KVH):
         for g in range(group_count):
@@ -662,29 +638,23 @@
             flat[...], out_w[c], NT, preferred_element_type=jnp.float32
         ).astype(jnp.bfloat16)
 
-    own_pages.wait()
-
-    row_copy(0, 0, me, partner).wait_send()
-    att_copy(0, 0, me, partner).wait_send()
+    results = [
+        pltpu.make_async_copy(src, dst, result_sem.at[i])
+        for i, (src, dst) in enumerate(
+            ((mixed_ref, mixed_hbm), (fresh_ref, fresh_hbm), (place_ref, place_hbm))
+        )
+    ]
+    for result in results:
+        result.start()
+    for result in results:
+        result.wait()
+    remote(arrived_hbm, arrived_hbm, page_send, page_recv, partner).wait_recv()
+    sent_pages = pages.at[pl.ds(0, (devices - 1) * capacity)]
+    remote(sent_pages, sent_pages, page_send, page_recv, partner).wait_send()
+    many_rows(devices - 1).wait_send()
+    many_parts(half - 1).wait_send()
     swap_copy().wait_send()
-
-    @pl.loop(1, half)
-    def _(offset):
-        for stage, owner in ((0, me), (1, partner)):
-            row_copy(stage, offset, owner, near(offset)).wait_send()
-            att_copy(stage, offset, owner, near(offset)).wait_send()
-        part_copy(offset, lax.rem(here + offset, half), here, near(offset)).wait_send()
-
-    for rank in range(capacity):
-        page_copy(rank, 0, partner).wait_send()
-        page_arrival(rank, 0, partner).wait_recv()
-
-        @pl.loop(1, half)
-        def _(offset):
-            page_copy(rank, offset, far(offset)).wait_send()
-            page_arrival(rank, offset, far_sender(offset)).wait_recv()
-            page_copy(rank, half + offset, near(offset)).wait_send()
-            page_arrival(rank, half + offset, near_sender(offset)).wait_recv()
+    many_att(half - 1).wait_send()
 
 
 def fused_body(hidden_states, qkv_weight, out_weight, cache_pages, context_lengths, new_units, old_pages):
@@ -715,7 +685,7 @@
             jax.ShapeDtypeStruct((2, pages_dev), i32),
         ),
         in_specs=[pl.BlockSpec(memory_space=pltpu.HBM)] * 7,
-        out_specs=(hbm, vmem, vmem, vmem),
+        out_specs=(hbm, hbm, hbm, hbm),
         scratch_shapes=[
             pltpu.SMEM(lengths.shape, i32),
             pltpu.SMEM(unit_table.shape, i32),
@@ -739,16 +709,20 @@
             pltpu.VMEM((KVH, rows, HD), bf16),
             pltpu.VMEM((devices // 2, 2, U_DEV + 1) + tile, bf16),
             pltpu.VMEM((devices // 2, 2, U_DEV + 1) + tile, bf16),
-            pltpu.VMEM((U_DEV + 1,) + tile, bf16),
-            pltpu.VMEM((U_DEV + 1,) + tile, bf16),
-            pltpu.VMEM((units,) + tile, bf16),
+            pltpu.VMEM((2 * (U_DEV + 1),) + tile, bf16),
+            pltpu.VMEM((2 * (U_DEV + 1),) + tile, bf16),
+            pltpu.VMEM((devices // 2, 2 * U_DEV) + tile, bf16),
             pltpu.VMEM((rows, HEADS * HD), bf16),
             dma((heads + tiles,)),
-            dma((capacity, devices)), dma((capacity, devices)),
-            dma((2, devices // 2)), dma((2, devices // 2)),
-            dma((devices // 2,)), dma((devices // 2,)),
-            dma((2, devices // 2)), dma((2, devices // 2)),
-            dma(()), dma((6,)), dma((1,)),
+            dma(()), dma(()),
+            dma(()), dma((2,)),
+            dma(()), dma(()), dma(()), dma(()),
+            dma(()), dma(()),
+            dma((6,)), dma((1,)),
+            pltpu.VMEM((rows, out_weight.shape[0]), bf16),
+            pltpu.VMEM((U_DEV, 2, 2 * HD), f32),
+            pltpu.VMEM((2, pages_dev), i32),
+            dma((3,)),
         ],
         compiler_params=pltpu.CompilerParams(
             collective_id=0, has_side_effects=True, vmem_limit_bytes=44 << 20
@@ -767,7 +741,7 @@
         scratch_shapes=[
             pltpu.VMEM((U_DEV, 2) + cache_pages.shape[1:], bf16),
             pltpu.VMEM(mixed_shape, bf16),
-            dma((pages_dev,)), dma(()),
+            dma(()), dma(()),
         ],
         compiler_params=pltpu.CompilerParams(vmem_limit_bytes=8 << 20),
         name="place_pages",

time: 113 us -> 103 us (0.912)
  the two profiles are of different devices: /device:TPU:1 before, /device:TPU:10 now
where the time goes in v2:
time: 103 us; the launch traced here: 102 us
  Pallas kernels  102 us (99%)
    pallas_call x1, Pallas kernels, fused_body(): pl.pallas_call(lambda *refs: layer_kernel(devices, capacity, *refs), out_...  99 us
    pallas_call x1, Pallas kernels, fused_body(): pl.pallas_call(place_kernel, out_shape=(jax.ShapeDtypeStruct(cache_pages....  2.54 us

profile of v2, /device:TPU:10, one launch (start us, length us, event | category | flops | bytes accessed | tf_op | source)
XLA Modules:
  0.0 102.2 jit_solution(6506444954568335734)
XLA Ops:
  0.6 99.0 %layer.1 = (bf16[64,128,256]{2,1,0:T(8,128)(2,1)S(1)}, bf16[16,512]{1,0:T(8,128)(2,1)S(1)}, f32[4,2,256]{2,1,0:T(2,128)S(1)}, s32[2,64]{1,0:T(2,128)S(1)}) custom-call(s32[1,8]{1,0:T(1,128)} %bitcast.4, s32[1,64]{1,0:T(1,128)} %bitcast.5, s32[8,128]{1,0:T(8,128)} %bitcast.3, bf16[8,2,8192]{2,1,0:T(2,128)(2,1)} %refs_3_.1, bf16[640,8192]{1,0:T(8,128)(2,1)} %refs_4_.1, ...), custom_call_target="tpu_custom_call" | custom-call | tf_op jit(solution)/shard_map/layer/pallas_call | solution.py:679
  99.7 2.5 %place_pages.1 = (bf16[64,128,256]{2,1,0:T(8,128)(2,1)}, bf16[8,2,512]{2,1,0:T(2,128)(2,1)}) custom-call(s32[2,64]{1,0:T(2,128)S(1)} %get-tuple-element.8.table_ref, bf16[64,128,256]{2,1,0:T(8,128)(2,1)S(1)} %get-tuple-element.9.arrived_ref, f32[4,2,256]{2,1,0:T(2,128)S(1)} %get-tuple-element.10.fresh_ref, bf16[16,512]{1,0:T(8,128)(2,1)S(1)} %get-tuple-element.11.mixed_ref), custom_call_target="tpu_custom_call" | custom-call | tf_op jit(solution)/shard_map/place_pages/pallas_call | solution.py:733

commit v3 on v2

--- a/solution.py
+++ b/solution.py
@@ -332,14 +332,6 @@
     lane = lax.broadcasted_iota(jnp.int32, (2 * group_count, PAGE), 1)
     strip = PAGE // U_DEV
 
-    barrier = pltpu.get_barrier_semaphore()
-
-    @pl.loop(1, devices)
-    def _(offset):
-        pl.semaphore_signal(
-            barrier, inc=1, device_id={"tp": lax.rem(me + offset, devices)}, device_id_type=pl.DeviceIdType.MESH
-        )
-
     small = [
         pltpu.make_async_copy(ids_hbm, ids, small_sem.at[0]),
         pltpu.make_async_copy(units_hbm, units_v, small_sem.at[1]),
@@ -360,6 +352,14 @@
     ]
     for load in small + [load_pages]:
         load.start()
+
+    barrier = pltpu.get_barrier_semaphore()
+
+    @pl.loop(1, devices)
+    def _(offset):
+        pl.semaphore_signal(
+            barrier, inc=1, device_id={"tp": lax.rem(me + offset, devices)}, device_id_type=pl.DeviceIdType.MESH
+        )
 
     def numbers(shape, axis):
         return lax.broadcasted_iota(jnp.int32, shape, axis)
@@ -420,12 +420,20 @@
         load.start()
     to_table.wait()
 
-    @pl.loop(0, pages_dev)
-    def _(i):
-        pages[i] = unsorted[table[in_order, i]]
-
+    def sort_page(at):
+        pages[at] = unsorted[table[in_order, at]]
+
+    def sort_turns(start, stop):
+        @pl.loop(start, stop)
+        def _(turn):
+            rank, place = turn // half, lax.rem(turn, half)
+            sort_page(far(place) * capacity + rank)
+            sort_page(near(place) * capacity + rank)
+
+    sort_turns(0, share(PLAN[0]))
     pl.semaphore_wait(barrier, devices - 1)
     send_pages(0, share(PLAN[0]))
+    sort_turns(share(PLAN[0]), turns)
 
     small[2].wait()
     row_at = lax.broadcasted_iota(jnp.int32, (rows, HD), 0)

time: 103 us -> 102 us (level)
  Pallas kernels: 102 us -> 100 us
    pallas_call x1, Pallas kernels: 99 us -> 97.8 us  [fused_body(): pl.pallas_call(lambda *refs: layer_kernel(devices, capacity, *refs), out_...]
where the time goes in v3:
time: 102 us; the launch traced here: 101 us
  Pallas kernels  100 us (98%)
    pallas_call x1, Pallas kernels, fused_body(): pl.pallas_call(lambda *refs: layer_kernel(devices, capacity, *refs), out_...  97.8 us
    pallas_call x1, Pallas kernels, fused_body(): pl.pallas_call(place_kernel, out_shape=(jax.ShapeDtypeStruct(cache_pages....  2.54 us

profile of v3, /device:TPU:10, one launch (start us, length us, event | category | flops | bytes accessed | tf_op | source)
XLA Modules:
  0.0 101.0 jit_solution(7539645666449593910)
XLA Ops:
  0.6 97.8 %layer.1 = (bf16[64,128,256]{2,1,0:T(8,128)(2,1)S(1)}, bf16[16,512]{1,0:T(8,128)(2,1)S(1)}, f32[4,2,256]{2,1,0:T(2,128)S(1)}, s32[2,64]{1,0:T(2,128)S(1)}) custom-call(s32[1,8]{1,0:T(1,128)} %bitcast.4, s32[1,64]{1,0:T(1,128)} %bitcast.5, s32[8,128]{1,0:T(8,128)} %bitcast.3, bf16[8,2,8192]{2,1,0:T(2,128)(2,1)} %refs_3_.1, bf16[640,8192]{1,0:T(8,128)(2,1)} %refs_4_.1, ...), custom_call_target="tpu_custom_call" | custom-call | tf_op jit(solution)/shard_map/layer/pallas_call | solution.py:687
  98.5 2.5 %place_pages.1 = (bf16[64,128,256]{2,1,0:T(8,128)(2,1)}, bf16[8,2,512]{2,1,0:T(2,128)(2,1)}) custom-call(s32[2,64]{1,0:T(2,128)S(1)} %get-tuple-element.8.table_ref, bf16[64,128,256]{2,1,0:T(8,128)(2,1)S(1)} %get-tuple-element.9.arrived_ref, f32[4,2,256]{2,1,0:T(2,128)S(1)} %get-tuple-element.10.fresh_ref, bf16[16,512]{1,0:T(8,128)(2,1)S(1)} %get-tuple-element.11.mixed_ref), custom_call_target="tpu_custom_call" | custom-call | tf_op jit(solution)/shard_map/place_pages/pallas_call | solution.py:741

commit v4 on v2

--- a/solution.py
+++ b/solution.py
@@ -228,17 +228,18 @@
 
 
 NT = (((1,), (1,)), ((), ()))
-PLAN = (4, 8, 12, 18, 24)
+PLAN = (8,12,16,22,28)
+FIRST = 32
 
 
 def layer_kernel(
     devices, capacity,
     lengths_hbm, units_hbm, ids_hbm, hidden_hbm, qkv_hbm, out_hbm, pages_hbm,
     arrived_hbm, mixed_hbm, fresh_hbm, place_hbm,
-    lengths, units_s, units_v, ids, tables_v, table, hidden_in, hidden_wide, hidden_ref, cos_ref, sin_ref,
-    qkv_w, out_w, unsorted, pages, rows_all, spread, queries, new_keys, new_values, part_out, part_in, swap_out, swap_in, att_all, flat,
+    lengths, units_s, units_v, ids, order_v, order, tables_v, table, hidden_in, hidden_wide, hidden_ref, cos_ref, sin_ref,
+    qkv_w, out_w, unsorted_head, unsorted_tail, pages, rows_all, spread, queries, new_keys, new_values, part_out, part_in, swap_out, swap_in, att_all, flat,
     load_sem, page_send, page_recv, row_send, row_recv, part_send, part_recv, swap_send, swap_recv, att_send, att_recv,
-    small_sem, table_sem, mixed_ref, fresh_ref, place_ref, result_sem,
+    small_sem, table_sem, settled, mixed_ref, fresh_ref, place_ref, result_sem,
 ):
     me = lax.axis_index("tp")
     pages_dev = pages.shape[0]
@@ -252,7 +253,7 @@
     head_rows = group_count + 2
     score_scale = 1.0 / math.sqrt(HD)
     span = requests * 2 * group_count
-    in_order, of_query, of_left, of_target, of_slot = range(5)
+    of_query, of_left, of_target, of_slot = range(4)
 
     half, quarter = devices // 2, devices // 4
     here, side = lax.rem(me, half), me // half
@@ -270,9 +271,10 @@
             device_id={"tp": device}, device_id_type=pl.DeviceIdType.MESH,
         )
 
-    def page_copy(rank, device):
+    def page_copy(rank, device, start=0, size=PAGE):
         return remote(
-            pages.at[device * capacity + rank], arrived_hbm.at[me * capacity + rank],
+            pages.at[device * capacity + rank, pl.ds(start, size)],
+            arrived_hbm.at[me * capacity + rank, pl.ds(start, size)],
             page_send, page_recv, device,
         )
 
@@ -305,15 +307,34 @@
 
     turns = half * capacity
 
+    def turn_of(turn):
+        rank, place = turn // half, lax.rem(turn, half)
+        if capacity == 1:
+            return rank, place
+        head = turn < 2 * half
+        rank = jnp.where(head, lax.rem(turn // quarter, 2), rank)
+        return rank, jnp.where(head, turn // half * quarter + lax.rem(turn, quarter), place)
+
+    def send_far(start, stop, *part):
+        @pl.loop(start, stop)
+        def _(turn):
+            rank, place = turn_of(turn)
+            page_copy(rank, far(place), *part).start()
+
+    def send_near(start, stop):
+        @pl.loop(start, stop)
+        def _(turn):
+            rank, place = turn_of(turn)
+
+            @pl.when(place > 0)
+            def _():
+                page_copy(rank, near(place)).start()
+
     def send_pages(start, stop):
         @pl.loop(start, stop)
         def _(turn):
-            rank, place = turn // half, lax.rem(turn, half)
-            page_copy(rank, far(place)).start()
-
-            @pl.when(place > 0)
-            def _():
-                page_copy(rank, near(place)).start()
+            send_far(turn, turn + 1)
+            send_near(turn, turn + 1)
 
     def share(numerator):
         return turns * numerator // 32
@@ -332,21 +353,18 @@
     lane = lax.broadcasted_iota(jnp.int32, (2 * group_count, PAGE), 1)
     strip = PAGE // U_DEV
 
-    barrier = pltpu.get_barrier_semaphore()
-
-    @pl.loop(1, devices)
-    def _(offset):
-        pl.semaphore_signal(
-            barrier, inc=1, device_id={"tp": lax.rem(me + offset, devices)}, device_id_type=pl.DeviceIdType.MESH
-        )
-
     small = [
         pltpu.make_async_copy(ids_hbm, ids, small_sem.at[0]),
         pltpu.make_async_copy(units_hbm, units_v, small_sem.at[1]),
         pltpu.make_async_copy(units_hbm, units_s, small_sem.at[2]),
         pltpu.make_async_copy(lengths_hbm, lengths, small_sem.at[3]),
     ]
-    load_pages = pltpu.make_async_copy(pages_hbm, unsorted, small_sem.at[4])
+    load_pages = [
+        pltpu.make_async_copy(
+            pages_hbm.at[:, pl.ds(start, part.shape[1])], part, small_sem.at[sem]
+        )
+        for start, part, sem in ((0, unsorted_head, 4), (FIRST, unsorted_tail, 6))
+    ]
     load_hidden = pltpu.make_async_copy(hidden_hbm, hidden_in, small_sem.at[5])
     loads = [
         pltpu.make_async_copy(qkv_hbm.at[pl.ds(c * HD, HD)], qkv_w.at[c], load_sem.at[c])
@@ -358,8 +376,27 @@
         )
         for c in range(tiles)
     ]
-    for load in small + [load_pages]:
+    for load in small + load_pages:
         load.start()
+
+    barrier = pltpu.get_barrier_semaphore()
+
+    def greet(semaphore, device):
+        pl.semaphore_signal(
+            semaphore, inc=1, device_id={"tp": device}, device_id_type=pl.DeviceIdType.MESH
+        )
+
+    @pl.when(side == 0)
+    def _():
+        @pl.loop(half, devices)
+        def _(device):
+            greet(barrier, device)
+
+    @pl.when(me // quarter == 2)
+    def _():
+        @pl.loop(0, half)
+        def _(device):
+            greet(barrier, device)
 
     def numbers(shape, axis):
         return lax.broadcasted_iota(jnp.int32, shape, axis)
@@ -392,7 +429,9 @@
     target_row = down(k_sub == k_lane, target_col)
     rank_col = across((target_col == target_row) & (k_lane < k_sub), jnp.ones(square, jnp.int32))
     sent = target_col * capacity + rank_col == k_lane
-    tables_v[in_order : in_order + 1, :] = index_row(down(sent, k_sub), pages_dev)
+    order_v[...] = index_row(down(sent, k_sub), pages_dev)
+    to_order = pltpu.make_async_copy(order_v, order, table_sem.at[1])
+    to_order.start()
     id_row = down(sent, id_col)
     tables_v[of_target : of_target + 1, :] = down(sent, slot_col - target_col * U_DEV)
     sent_unit = whole(id_row, per_unit)
@@ -415,17 +454,47 @@
     to_table = pltpu.make_async_copy(tables_v, table, table_sem.at[0])
     to_table.start()
 
-    load_pages.wait()
+    to_order.wait()
+
+    def sort_page(at, head=True, tail=True):
+        if head:
+            pages[at, pl.ds(0, FIRST)] = unsorted_head[order[0, at]]
+        if tail:
+            pages[at, pl.ds(FIRST, PAGE - FIRST)] = unsorted_tail[order[0, at]]
+
+    def sort_far(start, stop, *part):
+        @pl.loop(start, stop)
+        def _(turn):
+            rank, place = turn_of(turn)
+            sort_page(far(place) * capacity + rank, *part)
+
+    def sort_near(start, stop):
+        @pl.loop(start, stop)
+        def _(turn):
+            rank, place = turn_of(turn)
+            sort_page(near(place) * capacity + rank)
+
+    early = min(share(PLAN[0]), min(capacity, 2) * quarter)
+    load_pages[0].wait()
+    sort_far(0, early, True, False)
+    pl.semaphore_wait(barrier, jnp.where(side == 0, quarter, half))
+    send_far(0, early, 0, FIRST)
+    load_pages[1].wait()
+    sort_far(0, early, False, True)
+    send_far(0, early, FIRST, PAGE - FIRST)
     for load in [load_hidden] + loads[:heads]:
         load.start()
+
+    @pl.when(side == 1)
+    def _():
+        @pl.loop(0, half)
+        def _(device):
+            greet(settled, device)
+
+    sort_near(0, early)
+    sort_far(early, turns)
+    sort_near(early, turns)
     to_table.wait()
-
-    @pl.loop(0, pages_dev)
-    def _(i):
-        pages[i] = unsorted[table[in_order, i]]
-
-    pl.semaphore_wait(barrier, devices - 1)
-    send_pages(0, share(PLAN[0]))
 
     small[2].wait()
     row_at = lax.broadcasted_iota(jnp.int32, (rows, HD), 0)
@@ -443,6 +512,11 @@
         hidden_wide[2 * r : 2 * r + 2, :] = hidden_in[r].astype(jnp.float32)
     hidden_ref[...] = hidden_wide[...].astype(jnp.bfloat16)
 
+    @pl.when(side == 0)
+    def _():
+        pl.semaphore_wait(settled, half)
+        greet(settled, partner)
+
     for c in range(heads):
         loads[c].wait()
         part = lax.dot_general(
@@ -454,11 +528,22 @@
 
     row_copy(0, me, partner).start()
 
+    @pl.when(side == 1)
+    def _():
+        pl.semaphore_wait(settled, 1)
+
     @pl.loop(1, half)
     def _(offset):
         row_copy(1, me, near(offset)).start()
 
-    send_pages(share(PLAN[0]), share(PLAN[1]))
+    late = share(PLAN[1]) - early
+
+    @pl.loop(0, late)
+    def _(turn):
+        send_far(early + turn, early + turn + 1)
+        send_near(turn * early // late, (turn + 1) * early // late)
+
+    send_near(early, share(PLAN[1]))
     for load in loads[heads:]:
         load.start()
     own_pages = pltpu.make_async_copy(
@@ -691,6 +776,8 @@
             pltpu.SMEM(unit_table.shape, i32),
             pltpu.VMEM(unit_table.shape, i32),
             pltpu.VMEM(page_table.shape, i32),
+            pltpu.VMEM((1, pages_dev), i32),
+            pltpu.SMEM((1, pages_dev), i32),
             pltpu.VMEM((8, pages_dev), i32),
             pltpu.SMEM((8, pages_dev), i32),
             pltpu.VMEM(hidden_states.shape, bf16),
@@ -700,7 +787,8 @@
             pltpu.VMEM((rows, HD), f32),
             pltpu.VMEM((heads, HD, D), bf16),
             pltpu.VMEM((tiles, HD, HEADS * HD), bf16),
-            pltpu.VMEM(cache_pages.shape, bf16),
+            pltpu.VMEM((pages_dev, FIRST, 2 * HD), bf16),
+            pltpu.VMEM((pages_dev, PAGE - FIRST, 2 * HD), bf16),
             pltpu.VMEM(cache_pages.shape, bf16),
             pltpu.VMEM((devices, heads, rows, HD), bf16),
             pltpu.VMEM((units * 2 * group_count, HD), f32),
@@ -718,7 +806,7 @@
             dma(()), dma((2,)),
             dma(()), dma(()), dma(()), dma(()),
             dma(()), dma(()),
-            dma((6,)), dma((1,)),
+            dma((7,)), dma((2,)), pltpu.SemaphoreType.REGULAR,
             pltpu.VMEM((rows, out_weight.shape[0]), bf16),
             pltpu.VMEM((U_DEV, 2, 2 * HD), f32),
             pltpu.VMEM((2, pages_dev), i32),

time: 103 us -> 101 us (0.981)
  Pallas kernels: 102 us -> 99.8 us
    pallas_call x1, Pallas kernels: 99 us -> 97.3 us  [fused_body(): pl.pallas_call(lambda *refs: layer_kernel(devices, capacity, *refs), out_...]
where the time goes in v4:
time: 101 us; the launch traced here: 100 us
  Pallas kernels  99.8 us (99%)
    pallas_call x1, Pallas kernels, fused_body(): pl.pallas_call(lambda *refs: layer_kernel(devices, capacity, *refs), out_...  97.3 us
    pallas_call x1, Pallas kernels, fused_body(): pl.pallas_call(place_kernel, out_shape=(jax.ShapeDtypeStruct(cache_pages....  2.54 us

profile of v4, /device:TPU:10, one launch (start us, length us, event | category | flops | bytes accessed | tf_op | source)
XLA Modules:
  0.0 100.4 jit_solution(8174250901456160622)
XLA Ops:
  0.6 97.3 %layer.1 = (bf16[64,128,256]{2,1,0:T(8,128)(2,1)S(1)}, bf16[16,512]{1,0:T(8,128)(2,1)S(1)}, f32[4,2,256]{2,1,0:T(2,128)S(1)}, s32[2,64]{1,0:T(2,128)S(1)}) custom-call(s32[1,8]{1,0:T(1,128)} %bitcast.4, s32[1,64]{1,0:T(1,128)} %bitcast.5, s32[8,128]{1,0:T(8,128)} %bitcast.3, bf16[8,2,8192]{2,1,0:T(2,128)(2,1)} %refs_3_.1, bf16[640,8192]{1,0:T(8,128)(2,1)} %refs_4_.1, ...), custom_call_target="tpu_custom_call" | custom-call | tf_op jit(solution)/shard_map/layer/pallas_call | solution.py:764
  97.9 2.5 %place_pages.1 = (bf16[64,128,256]{2,1,0:T(8,128)(2,1)}, bf16[8,2,512]{2,1,0:T(2,128)(2,1)}) custom-call(s32[2,64]{1,0:T(2,128)S(1)} %get-tuple-element.8.table_ref, bf16[64,128,256]{2,1,0:T(8,128)(2,1)S(1)} %get-tuple-element.9.arrived_ref, f32[4,2,256]{2,1,0:T(2,128)S(1)} %get-tuple-element.10.fresh_ref, bf16[16,512]{1,0:T(8,128)(2,1)S(1)} %get-tuple-element.11.mixed_ref), custom_call_target="tpu_custom_call" | custom-call | tf_op jit(solution)/shard_map/place_pages/pallas_call | solution.py:821

commit v5 on v4

--- a/solution.py
+++ b/solution.py
@@ -263,7 +263,7 @@
         return side * half + lax.rem(here + offset, half)
 
     def far(turn):
-        return (1 - side) * half + (turn // quarter) * quarter + lax.rem(turn + me, quarter)
+        return (1 - side) * half + (turn // quarter) * quarter + lax.rem(turn + me + 1, quarter)
 
     def remote(src, dst, send, recv, device):
         return pltpu.make_async_remote_copy(
@@ -340,6 +340,7 @@
         return turns * numerator // 32
 
     def pack_totals(values):
+        strip = PAGE // len(values)
         packed = jnp.zeros((2 * group_count, PAGE), jnp.float32)
         for j, total in enumerate(values):
             top = total.astype(jnp.bfloat16).astype(jnp.float32)
@@ -347,11 +348,10 @@
             packed = jnp.where(lane == j * strip + strip // 2, total - top, packed)
         return packed.astype(jnp.bfloat16)
 
-    def unpack_total(packed, j):
-        return jnp.sum(jnp.where(lane // strip == j, packed, 0.0), axis=-1, keepdims=True)
+    def unpack_total(packed, j, count=U_DEV):
+        return jnp.sum(jnp.where(lane // (PAGE // count) == j, packed, 0.0), axis=-1, keepdims=True)
 
     lane = lax.broadcasted_iota(jnp.int32, (2 * group_count, PAGE), 1)
-    strip = PAGE // U_DEV
 
     small = [
         pltpu.make_async_copy(ids_hbm, ids, small_sem.at[0]),
@@ -587,21 +587,25 @@
         )
         zero = jnp.zeros((2 * group_count, PAGE), jnp.float32)
         sums, totals = [zero] * U_DEV, [zero[:, :1]] * U_DEV
-        for rank in range(capacity):
-            query = queries[table[of_query, target * capacity + rank]]
-            left = table[of_left, target * capacity + rank]
-            page = pages[target * capacity + rank]
-            scores = lax.dot_general(
-                query, page[:, :HD], NT, preferred_element_type=jnp.float32
+        places = [target * capacity + rank for rank in range(capacity)]
+        scores = [
+            lax.dot_general(
+                queries[table[of_query, at]], pages[at, :, :HD], NT, preferred_element_type=jnp.float32
             ) * score_scale
-            weights = jnp.where(lane < left, jnp.exp(scores), 0.0)
-            total = jnp.sum(weights, axis=-1, keepdims=True)
-            weighted = jnp.dot(
-                weights.astype(jnp.bfloat16), page[:, HD:], preferred_element_type=jnp.float32
-            )
-            slot = table[of_target, target * capacity + rank]
+            for at in places
+        ]
+        weights = [
+            jnp.where(lane < table[of_left, at], jnp.exp(score), 0.0)
+            for at, score in zip(places, scores)
+        ]
+        weighted = [
+            jnp.dot(weight.astype(jnp.bfloat16), pages[at, :, HD:], preferred_element_type=jnp.float32)
+            for at, weight in zip(places, weights)
+        ]
+        for at, weight, added in zip(places, weights, weighted):
+            slot, total = table[of_target, at], jnp.sum(weight, axis=-1, keepdims=True)
             for j in range(U_DEV):
-                sums[j] = sums[j] + jnp.where(slot == j, weighted, 0.0)
+                sums[j] = sums[j] + jnp.where(slot == j, added, 0.0)
                 totals[j] = totals[j] + jnp.where(slot == j, total, 0.0)
         place, which = lax.rem(target, half), target // half
         for j in range(U_DEV):
@@ -677,26 +681,20 @@
         )
         return lax.fori_loop(1, half, add, first)
 
-    kept = half_sum(0) + half_sum(1)
-    blocks = U_DEV + 1
-    for which in range(2):
-        for j in range(U_DEV):
-            swap_out[which * blocks + j] = kept[which * blocks + j].astype(jnp.bfloat16)
-        packed = kept[which * blocks + U_DEV]
-        swap_out[which * blocks + U_DEV] = pack_totals(
-            [unpack_total(packed, j) for j in range(U_DEV)]
-        )
+    halves = [half_sum(0), half_sum(1)]
+    kept = [block for halved in halves for block in halved[:U_DEV]]
+    kept_totals = [unpack_total(halved[U_DEV], j) for halved in halves for j in range(U_DEV)]
+    for j in range(2 * U_DEV):
+        swap_out[j] = kept[j].astype(jnp.bfloat16)
+    swap_out[2 * U_DEV] = pack_totals(kept_totals)
     swap_copy().start()
     send_pages(share(PLAN[3]), share(PLAN[4]))
     swap_copy().wait_recv()
-    for which in range(2):
-        last = which * blocks + U_DEV
-        packed = kept[last] + swap_in[last].astype(jnp.float32)
-        for j in range(U_DEV):
-            at = which * blocks + j
-            total = own_totals[which * U_DEV + j] + unpack_total(packed, j)
-            weighted = own_sums[which * U_DEV + j] + kept[at] + swap_in[at].astype(jnp.float32)
-            att_all[here, which * U_DEV + j] = (weighted / total).astype(jnp.bfloat16)
+    packed = swap_in[2 * U_DEV].astype(jnp.float32)
+    for j in range(2 * U_DEV):
+        total = own_totals[j] + kept_totals[j] + unpack_total(packed, j, 2 * U_DEV)
+        weighted = own_sums[j] + kept[j] + swap_in[j].astype(jnp.float32)
+        att_all[here, j] = (weighted / total).astype(jnp.bfloat16)
 
     @pl.loop(1, half)
     def _(offset):
@@ -797,8 +795,8 @@
             pltpu.VMEM((KVH, rows, HD), bf16),
             pltpu.VMEM((devices // 2, 2, U_DEV + 1) + tile, bf16),
             pltpu.VMEM((devices // 2, 2, U_DEV + 1) + tile, bf16),
-            pltpu.VMEM((2 * (U_DEV + 1),) + tile, bf16),
-            pltpu.VMEM((2 * (U_DEV + 1),) + tile, bf16),
+            pltpu.VMEM((2 * U_DEV + 1,) + tile, bf16),
+            pltpu.VMEM((2 * U_DEV + 1,) + tile, bf16),
             pltpu.VMEM((devices // 2, 2 * U_DEV) + tile, bf16),
             pltpu.VMEM((rows, HEADS * HD), bf16),
             dma((heads + tiles,)),

time: 101 us -> 100 us (0.990)
  no operation moved by 1% of the time
where the time goes in v5:
time: 100 us
  Pallas kernels  99.4 us (99%)
    pallas_call x1, Pallas kernels, fused_body(): pl.pallas_call(lambda *refs: layer_kernel(devices, capacity, *refs), out_...  96.8 us
    pallas_call x1, Pallas kernels, fused_body(): pl.pallas_call(place_kernel, out_shape=(jax.ShapeDtypeStruct(cache_pages....  2.54 us

profile of v5, /device:TPU:10, one launch (start us, length us, event | category | flops | bytes accessed | tf_op | source)
XLA Modules:
  0.0 100.0 jit_solution(5971145527407772209)
XLA Ops:
  0.6 96.8 %layer.1 = (bf16[64,128,256]{2,1,0:T(8,128)(2,1)S(1)}, bf16[16,512]{1,0:T(8,128)(2,1)S(1)}, f32[4,2,256]{2,1,0:T(2,128)S(1)}, s32[2,64]{1,0:T(2,128)S(1)}) custom-call(s32[1,8]{1,0:T(1,128)} %bitcast.4, s32[1,64]{1,0:T(1,128)} %bitcast.5, s32[8,128]{1,0:T(8,128)} %bitcast.3, bf16[8,2,8192]{2,1,0:T(2,128)(2,1)} %refs_3_.1, bf16[640,8192]{1,0:T(8,128)(2,1)} %refs_4_.1, ...), custom_call_target="tpu_custom_call" | custom-call | tf_op jit(solution)/shard_map/layer/pallas_call | solution.py:762
  97.5 2.5 %place_pages.1 = (bf16[64,128,256]{2,1,0:T(8,128)(2,1)}, bf16[8,2,512]{2,1,0:T(2,128)(2,1)}) custom-call(s32[2,64]{1,0:T(2,128)S(1)} %get-tuple-element.8.table_ref, bf16[64,128,256]{2,1,0:T(8,128)(2,1)S(1)} %get-tuple-element.9.arrived_ref, f32[4,2,256]{2,1,0:T(2,128)S(1)} %get-tuple-element.10.fresh_ref, bf16[16,512]{1,0:T(8,128)(2,1)S(1)} %get-tuple-element.11.mixed_ref), custom_call_target="tpu_custom_call" | custom-call | tf_op jit(solution)/shard_map/place_pages/pallas_call | solution.py:819

commit v6 on v5

--- a/solution.py
+++ b/solution.py
@@ -191,31 +191,23 @@
     def outward(at, src):
         return pltpu.make_async_copy(src, out_ref.at[at], sem)
 
-    def place_of(slot, page):
-        return slot * per_unit + lax.rem(table_ref[1, slot] // PAGE + page, per_unit)
-
     for slot in range(U_DEV):
         for page in range(steps, per_unit):
-            at = place_of(slot, page)
-            outward(at, arrived_ref.at[table_ref[0, at]]).start()
+            k = slot * per_unit + page
+            outward(table_ref[0, k], arrived_ref.at[table_ref[1, k]]).start()
 
     for slot in range(U_DEV):
         for page in range(steps):
-            at = place_of(slot, page)
+            k = slot * per_unit + page
+            at = table_ref[0, k]
             block = patched.at[slot, page]
-            block[...] = arrived_ref[table_ref[0, at]]
+            content = arrived_ref[table_ref[1, k]].astype(jnp.float32)
+            line = lax.broadcasted_iota(jnp.int32, content.shape, 0)
+            row = jnp.broadcast_to(table_ref[2:3, k : k + 1], content.shape)
             for step in range(steps):
-                row = table_ref[1, slot] + step - (at - slot * per_unit) * PAGE
-
-                @pl.when((row >= 0) & (row < PAGE))
-                def _():
-                    base = pl.multiple_of((row // 16) * 16, 16)
-                    tile = block[pl.ds(base, 16), :]
-                    line = lax.broadcasted_iota(jnp.int32, tile.shape, 0)
-                    new = jnp.broadcast_to(fresh_ref[slot, step : step + 1, :], tile.shape)
-                    mixed = jnp.where(line == row - base, new, tile.astype(jnp.float32))
-                    block[pl.ds(base, 16), :] = mixed.astype(jnp.bfloat16)
-
+                new = jnp.broadcast_to(fresh_ref[slot, step : step + 1, :], content.shape)
+                content = jnp.where(line == row + step, new, content)
+            block[...] = content.astype(jnp.bfloat16)
             outward(at, block).start()
 
     mixed = mixed_ref[...].astype(jnp.float32)
@@ -228,7 +220,7 @@
 
 
 NT = (((1,), (1,)), ((), ()))
-PLAN = (8,12,16,22,28)
+PLAN = (8,14,18,22,28)
 FIRST = 32
 
 
@@ -454,13 +446,12 @@
     to_table = pltpu.make_async_copy(tables_v, table, table_sem.at[0])
     to_table.start()
 
-    to_order.wait()
-
-    def sort_page(at, head=True, tail=True):
+    def sort_page(at, head=True, tail=True, source=None):
+        source = order[0, at] if source is None else source
         if head:
-            pages[at, pl.ds(0, FIRST)] = unsorted_head[order[0, at]]
+            pages[at, pl.ds(0, FIRST)] = unsorted_head[source]
         if tail:
-            pages[at, pl.ds(FIRST, PAGE - FIRST)] = unsorted_tail[order[0, at]]
+            pages[at, pl.ds(FIRST, PAGE - FIRST)] = unsorted_tail[source]
 
     def sort_far(start, stop, *part):
         @pl.loop(start, stop)
@@ -476,10 +467,15 @@
 
     early = min(share(PLAN[0]), min(capacity, 2) * quarter)
     load_pages[0].wait()
-    sort_far(0, early, True, False)
+    order_row = index_row(down(sent, k_sub), pages_dev)
+    for turn in range(early):
+        rank, place = turn_of(turn)
+        at = far(place) * capacity + rank
+        sort_page(at, True, False, jnp.sum(jnp.where(k_lane[0:1] == at, order_row, 0)))
     pl.semaphore_wait(barrier, jnp.where(side == 0, quarter, half))
     send_far(0, early, 0, FIRST)
     load_pages[1].wait()
+    to_order.wait()
     sort_far(0, early, False, True)
     send_far(0, early, FIRST, PAGE - FIRST)
     for load in [load_hidden] + loads[:heads]:
@@ -658,16 +654,20 @@
     rank_col = across(
         (holder_col == holder_row) & (source_row < source_col), jnp.ones(square, jnp.int32)
     )
-    place_ref[0:1, :] = index_row(
-        down(k_sub == k_lane, holder_col * capacity + rank_col), pages_dev
-    )
+    arrives_col = jnp.clip(holder_col * capacity + rank_col, 0, pages_dev - 1)
+    lane_row = numbers((1, pages_dev), 1)
+    slot_row = whole(lane_row, per_unit)
     own_lengths = jnp.zeros((1, pages_dev), jnp.int32)
     for j in range(U_DEV):
         own_lengths = jnp.where(
-            lax.broadcasted_iota(jnp.int32, (1, pages_dev), 1) == j,
-            lengths[0, units_s[0, me * U_DEV + j] // KVH], own_lengths,
-        )
-    place_ref[1:2, :] = own_lengths
+            slot_row == j, lengths[0, units_s[0, me * U_DEV + j] // KVH], own_lengths
+        )
+    turned = whole(own_lengths, PAGE) + lane_row - slot_row * per_unit
+    turned = turned - whole(turned, per_unit) * per_unit
+    place_row = slot_row * per_unit + turned
+    place_ref[0:1, :] = place_row
+    place_ref[1:2, :] = down(k_sub == place_row, arrives_col)
+    place_ref[2:3, :] = own_lengths - turned * PAGE
 
     many_parts(half - 1).wait_recv()
 
@@ -765,7 +765,7 @@
             jax.ShapeDtypeStruct(cache_pages.shape, bf16),
             jax.ShapeDtypeStruct((rows, out_weight.shape[0]), bf16),
             jax.ShapeDtypeStruct((U_DEV, 2, 2 * HD), f32),
-            jax.ShapeDtypeStruct((2, pages_dev), i32),
+            jax.ShapeDtypeStruct((3, pages_dev), i32),
         ),
         in_specs=[pl.BlockSpec(memory_space=pltpu.HBM)] * 7,
         out_specs=(hbm, hbm, hbm, hbm),
@@ -807,7 +807,7 @@
             dma((7,)), dma((2,)), pltpu.SemaphoreType.REGULAR,
             pltpu.VMEM((rows, out_weight.shape[0]), bf16),
             pltpu.VMEM((U_DEV, 2, 2 * HD), f32),
-            pltpu.VMEM((2, pages_dev), i32),
+            pltpu.VMEM((3, pages_dev), i32),
             dma((3,)),
         ],
         compiler_params=pltpu.CompilerParams(
@@ -822,7 +822,7 @@
             jax.ShapeDtypeStruct(cache_pages.shape, bf16),
             jax.ShapeDtypeStruct(mixed_shape, bf16),
         ),
-        in_specs=[smem, vmem, vmem, vmem],
+        in_specs=[vmem, vmem, vmem, vmem],
         out_specs=(hbm, hbm),
         scratch_shapes=[
             pltpu.VMEM((U_DEV, 2) + cache_pages.shape[1:], bf16),

time: 100 us -> 99.6 us (level)
  no operation moved by 1% of the time
where the time goes in v6:
time: 99.6 us; the launch traced here: 99.5 us
  Pallas kernels  98.8 us (99%)
    pallas_call x1, Pallas kernels, fused_body(): pl.pallas_call(lambda *refs: layer_kernel(devices, capacity, *refs), out_...  96.7 us
    pallas_call x1, Pallas kernels, fused_body(): pl.pallas_call(place_kernel, out_shape=(jax.ShapeDtypeStruct(cache_pages....  2.08 us

profile of v6, /device:TPU:10, one launch (start us, length us, event | category | flops | bytes accessed | tf_op | source)
XLA Modules:
  0.0 99.5 jit_solution(14802693448759061101)
XLA Ops:
  0.6 96.7 %layer.1 = (bf16[64,128,256]{2,1,0:T(8,128)(2,1)S(1)}, bf16[16,512]{1,0:T(8,128)(2,1)S(1)}, f32[4,2,256]{2,1,0:T(2,128)S(1)}, s32[3,64]{1,0:T(4,128)S(1)}) custom-call(s32[1,8]{1,0:T(1,128)} %bitcast.4, s32[1,64]{1,0:T(1,128)} %bitcast.5, s32[8,128]{1,0:T(8,128)} %bitcast.3, bf16[8,2,8192]{2,1,0:T(2,128)(2,1)} %refs_3_.1, bf16[640,8192]{1,0:T(8,128)(2,1)} %refs_4_.1, ...), custom_call_target="tpu_custom_call" | custom-call | tf_op jit(solution)/shard_map/layer/pallas_call | solution.py:762
  97.4 2.1 %place_pages.1 = (bf16[64,128,256]{2,1,0:T(8,128)(2,1)}, bf16[8,2,512]{2,1,0:T(2,128)(2,1)}) custom-call(s32[3,64]{1,0:T(4,128)S(1)} %get-tuple-element.8.table_ref, bf16[64,128,256]{2,1,0:T(8,128)(2,1)S(1)} %get-tuple-element.9.arrived_ref, f32[4,2,256]{2,1,0:T(2,128)S(1)} %get-tuple-element.10.fresh_ref, bf16[16,512]{1,0:T(8,128)(2,1)S(1)} %get-tuple-element.11.mixed_ref), custom_call_target="tpu_custom_call" | custom-call | tf_op jit(solution)/shard_map/place_pages/pallas_call | solution.py:819

commit v7 on v6

--- a/solution.py
+++ b/solution.py
@@ -221,7 +221,7 @@
 
 NT = (((1,), (1,)), ((), ()))
 PLAN = (8,14,18,22,28)
-FIRST = 32
+FIRST = 16
 
 
 def layer_kernel(
@@ -231,7 +231,7 @@
     lengths, units_s, units_v, ids, order_v, order, tables_v, table, hidden_in, hidden_wide, hidden_ref, cos_ref, sin_ref,
     qkv_w, out_w, unsorted_head, unsorted_tail, pages, rows_all, spread, queries, new_keys, new_values, part_out, part_in, swap_out, swap_in, att_all, flat,
     load_sem, page_send, page_recv, row_send, row_recv, part_send, part_recv, swap_send, swap_recv, att_send, att_recv,
-    small_sem, table_sem, settled, mixed_ref, fresh_ref, place_ref, result_sem,
+    small_sem, table_sem, settled, mixed_ref, fresh_ref, place_ref,
 ):
     me = lax.axis_index("tp")
     pages_dev = pages.shape[0]
@@ -364,7 +364,7 @@
     ]
     loads += [
         pltpu.make_async_copy(
-            out_hbm.at[pl.ds(c * HD, HD)], out_w.at[c], load_sem.at[heads + c]
+            out_hbm.at[pl.ds(c * HD, HD)], out_w.at[c], load_sem.at[c]
         )
         for c in range(tiles)
     ]
@@ -388,7 +388,7 @@
     def _():
         @pl.loop(0, half)
         def _(device):
-            greet(barrier, device)
+            greet(barrier, half - 1 - device)
 
     def numbers(shape, axis):
         return lax.broadcasted_iota(jnp.int32, shape, axis)
@@ -424,28 +424,6 @@
     order_v[...] = index_row(down(sent, k_sub), pages_dev)
     to_order = pltpu.make_async_copy(order_v, order, table_sem.at[1])
     to_order.start()
-    id_row = down(sent, id_col)
-    tables_v[of_target : of_target + 1, :] = down(sent, slot_col - target_col * U_DEV)
-    sent_unit = whole(id_row, per_unit)
-    sent_request = whole(sent_unit, KVH)
-    small[3].wait()
-    sent_length = jnp.zeros_like(id_row)
-    for r in range(requests):
-        sent_length = jnp.where(sent_request == r, lengths[0, r], sent_length)
-    tables_v[of_query : of_query + 1, :] = index_row(
-        (sent_unit - sent_request * KVH) * requests + sent_request, units
-    )
-    tables_v[of_left : of_left + 1, :] = sent_length - (id_row - sent_unit * per_unit) * PAGE
-    u_square = (units, units)
-    u_sub, u_lane = numbers(u_square, 0), numbers(u_square, 1)
-    unit_col = across(u_sub == u_lane, unit_row)
-    u_device = whole(u_sub, U_DEV)
-    u_side = whole(u_device, half)
-    u_place = (u_device - u_side * half) * (2 * U_DEV) + u_side * U_DEV + (u_sub - u_device * U_DEV)
-    tables_v[of_slot : of_slot + 1, :] = index_row(down(unit_col == u_lane, u_place), units)
-    to_table = pltpu.make_async_copy(tables_v, table, table_sem.at[0])
-    to_table.start()
-
     def sort_page(at, head=True, tail=True, source=None):
         source = order[0, at] if source is None else source
         if head:
@@ -478,6 +456,28 @@
     to_order.wait()
     sort_far(0, early, False, True)
     send_far(0, early, FIRST, PAGE - FIRST)
+    id_row = down(sent, id_col)
+    tables_v[of_target : of_target + 1, :] = down(sent, slot_col - target_col * U_DEV)
+    sent_unit = whole(id_row, per_unit)
+    sent_request = whole(sent_unit, KVH)
+    small[3].wait()
+    sent_length = jnp.zeros_like(id_row)
+    for r in range(requests):
+        sent_length = jnp.where(sent_request == r, lengths[0, r], sent_length)
+    tables_v[of_query : of_query + 1, :] = index_row(
+        (sent_unit - sent_request * KVH) * requests + sent_request, units
+    )
+    tables_v[of_left : of_left + 1, :] = sent_length - (id_row - sent_unit * per_unit) * PAGE
+    u_square = (units, units)
+    u_sub, u_lane = numbers(u_square, 0), numbers(u_square, 1)
+    unit_col = across(u_sub == u_lane, unit_row)
+    u_device = whole(u_sub, U_DEV)
+    u_side = whole(u_device, half)
+    u_place = (u_device - u_side * half) * (2 * U_DEV) + u_side * U_DEV + (u_sub - u_device * U_DEV)
+    tables_v[of_slot : of_slot + 1, :] = index_row(down(unit_col == u_lane, u_place), units)
+    to_table = pltpu.make_async_copy(tables_v, table, table_sem.at[0])
+    to_table.start()
+
     for load in [load_hidden] + loads[:heads]:
         load.start()
 
@@ -722,7 +722,7 @@
         ).astype(jnp.bfloat16)
 
     results = [
-        pltpu.make_async_copy(src, dst, result_sem.at[i])
+        pltpu.make_async_copy(src, dst, small_sem.at[i])
         for i, (src, dst) in enumerate(
             ((mixed_ref, mixed_hbm), (fresh_ref, fresh_hbm), (place_ref, place_hbm))
         )
@@ -799,7 +799,7 @@
             pltpu.VMEM((2 * U_DEV + 1,) + tile, bf16),
             pltpu.VMEM((devices // 2, 2 * U_DEV) + tile, bf16),
             pltpu.VMEM((rows, HEADS * HD), bf16),
-            dma((heads + tiles,)),
+            dma((max(heads, tiles),)),
             dma(()), dma(()),
             dma(()), dma((2,)),
             dma(()), dma(()), dma(()), dma(()),
@@ -808,7 +808,6 @@
             pltpu.VMEM((rows, out_weight.shape[0]), bf16),
             pltpu.VMEM((U_DEV, 2, 2 * HD), f32),
             pltpu.VMEM((3, pages_dev), i32),
-            dma((3,)),
         ],
         compiler_params=pltpu.CompilerParams(
             collective_id=0, has_side_effects=True, vmem_limit_bytes=44 << 20

time: 99.6 us -> 99.6 us (level)
  no operation moved by 1% of the time
where the time goes in v7:
time: 99.6 us; the launch traced here: 99.4 us
  Pallas kernels  98.8 us (99%)
    pallas_call x1, Pallas kernels, fused_body(): pl.pallas_call(lambda *refs: layer_kernel(devices, capacity, *refs), out_...  96.7 us
    pallas_call x1, Pallas kernels, fused_body(): pl.pallas_call(place_kernel, out_shape=(jax.ShapeDtypeStruct(cache_pages....  2.08 us

profile of v7, /device:TPU:10, one launch (start us, length us, event | category | flops | bytes accessed | tf_op | source)
XLA Modules:
  0.0 99.4 jit_solution(9911130401787219891)
XLA Ops:
  0.6 96.7 %layer.1 = (bf16[64,128,256]{2,1,0:T(8,128)(2,1)S(1)}, bf16[16,512]{1,0:T(8,128)(2,1)S(1)}, f32[4,2,256]{2,1,0:T(2,128)S(1)}, s32[3,64]{1,0:T(4,128)S(1)}) custom-call(s32[1,8]{1,0:T(1,128)} %bitcast.4, s32[1,64]{1,0:T(1,128)} %bitcast.5, s32[8,128]{1,0:T(8,128)} %bitcast.3, bf16[8,2,8192]{2,1,0:T(2,128)(2,1)} %refs_3_.1, bf16[640,8192]{1,0:T(8,128)(2,1)} %refs_4_.1, ...), custom_call_target="tpu_custom_call" | custom-call | tf_op jit(solution)/shard_map/layer/pallas_call | solution.py:762
  97.3 2.1 %place_pages.1 = (bf16[64,128,256]{2,1,0:T(8,128)(2,1)}, bf16[8,2,512]{2,1,0:T(2,128)(2,1)}) custom-call(s32[3,64]{1,0:T(4,128)S(1)} %get-tuple-element.8.table_ref, bf16[64,128,256]{2,1,0:T(8,128)(2,1)S(1)} %get-tuple-element.9.arrived_ref, f32[4,2,256]{2,1,0:T(2,128)S(1)} %get-tuple-element.10.fresh_ref, bf16[16,512]{1,0:T(8,128)(2,1)S(1)} %get-tuple-element.11.mixed_ref), custom_call_target="tpu_custom_call" | custom-call | tf_op jit(solution)/shard_map/place_pages/pallas_call | solution.py:818

commit v8 on v7

--- a/solution.py
+++ b/solution.py
@@ -220,7 +220,7 @@
 
 
 NT = (((1,), (1,)), ((), ()))
-PLAN = (8,14,18,22,28)
+PLAN = (8,15,19,23,28)
 FIRST = 16
 
 

time: 99.6 us -> 99.6 us (level)
  no operation moved by 1% of the time
where the time goes in v8:
time: 99.6 us; the launch traced here: 99.4 us
  Pallas kernels  98.8 us (99%)
    pallas_call x1, Pallas kernels, fused_body(): pl.pallas_call(lambda *refs: layer_kernel(devices, capacity, *refs), out_...  96.7 us
    pallas_call x1, Pallas kernels, fused_body(): pl.pallas_call(place_kernel, out_shape=(jax.ShapeDtypeStruct(cache_pages....  2.08 us

profile of v8, /device:TPU:10, one launch (start us, length us, event | category | flops | bytes accessed | tf_op | source)
XLA Modules:
  0.0 99.4 jit_solution(11103349963666306449)
XLA Ops:
  0.6 96.7 %layer.1 = (bf16[64,128,256]{2,1,0:T(8,128)(2,1)S(1)}, bf16[16,512]{1,0:T(8,128)(2,1)S(1)}, f32[4,2,256]{2,1,0:T(2,128)S(1)}, s32[3,64]{1,0:T(4,128)S(1)}) custom-call(s32[1,8]{1,0:T(1,128)} %bitcast.4, s32[1,64]{1,0:T(1,128)} %bitcast.5, s32[8,128]{1,0:T(8,128)} %bitcast.3, bf16[8,2,8192]{2,1,0:T(2,128)(2,1)} %refs_3_.1, bf16[640,8192]{1,0:T(8,128)(2,1)} %refs_4_.1, ...), custom_call_target="tpu_custom_call" | custom-call | tf_op jit(solution)/shard_map/layer/pallas_call | solution.py:762
  97.4 2.1 %place_pages.1 = (bf16[64,128,256]{2,1,0:T(8,128)(2,1)}, bf16[8,2,512]{2,1,0:T(2,128)(2,1)}) custom-call(s32[3,64]{1,0:T(4,128)S(1)} %get-tuple-element.8.table_ref, bf16[64,128,256]{2,1,0:T(8,128)(2,1)S(1)} %get-tuple-element.9.arrived_ref, f32[4,2,256]{2,1,0:T(2,128)S(1)} %get-tuple-element.10.fresh_ref, bf16[16,512]{1,0:T(8,128)(2,1)S(1)} %get-tuple-element.11.mixed_ref), custom_call_target="tpu_custom_call" | custom-call | tf_op jit(solution)/shard_map/place_pages/pallas_call | solution.py:818

commit v9 on v8

--- a/solution.py
+++ b/solution.py
@@ -220,7 +220,7 @@
 
 
 NT = (((1,), (1,)), ((), ()))
-PLAN = (8,15,19,23,28)
+PLAN = (8,16,20,24,29)
 FIRST = 16
 
 

time: 99.6 us -> 99.6 us (level)
  no operation moved by 1% of the time
where the time goes in v9:
time: 99.6 us; the launch traced here: 99.4 us
  Pallas kernels  98.8 us (99%)
    pallas_call x1, Pallas kernels, fused_body(): pl.pallas_call(lambda *refs: layer_kernel(devices, capacity, *refs), out_...  96.7 us
    pallas_call x1, Pallas kernels, fused_body(): pl.pallas_call(place_kernel, out_shape=(jax.ShapeDtypeStruct(cache_pages....  2.08 us

profile of v9, /device:TPU:10, one launch (start us, length us, event | category | flops | bytes accessed | tf_op | source)
XLA Modules:
  0.0 99.4 jit_solution(16470068072900808787)
XLA Ops:
  0.6 96.7 %layer.1 = (bf16[64,128,256]{2,1,0:T(8,128)(2,1)S(1)}, bf16[16,512]{1,0:T(8,128)(2,1)S(1)}, f32[4,2,256]{2,1,0:T(2,128)S(1)}, s32[3,64]{1,0:T(4,128)S(1)}) custom-call(s32[1,8]{1,0:T(1,128)} %bitcast.4, s32[1,64]{1,0:T(1,128)} %bitcast.5, s32[8,128]{1,0:T(8,128)} %bitcast.3, bf16[8,2,8192]{2,1,0:T(2,128)(2,1)} %refs_3_.1, bf16[640,8192]{1,0:T(8,128)(2,1)} %refs_4_.1, ...), custom_call_target="tpu_custom_call" | custom-call | tf_op jit(solution)/shard_map/layer/pallas_call | solution.py:762
  97.3 2.1 %place_pages.1 = (bf16[64,128,256]{2,1,0:T(8,128)(2,1)}, bf16[8,2,512]{2,1,0:T(2,128)(2,1)}) custom-call(s32[3,64]{1,0:T(4,128)S(1)} %get-tuple-element.8.table_ref, bf16[64,128,256]{2,1,0:T(8,128)(2,1)S(1)} %get-tuple-element.9.arrived_ref, f32[4,2,256]{2,1,0:T(2,128)S(1)} %get-tuple-element.10.fresh_ref, bf16[16,512]{1,0:T(8,128)(2,1)S(1)} %get-tuple-element.11.mixed_ref), custom_call_target="tpu_custom_call" | custom-call | tf_op jit(solution)/shard_map/place_pages/pallas_call | solution.py:818
